TPU v7x, 128 devices: a whole 4x4x4 slice. The times are simulated.
128 devices in a mesh: dp: 4 (over y_lo, core), ctx: 32 (over z, x, y_hi).
Axes of the slice: x: 4, y: 4 (y_hi: 2, y_lo: 2; y = y_hi * 2 + y_lo), z: 4, core: 2. Of those that a mesh axis runs over, the one named last changes fastest.
Arguments:
- queries: bfloat16 [4, 32768, 1024], P('dp', 'ctx'), may hold values from -160 to 160
- keys: bfloat16 [4, 32768, 1024], P('dp', 'ctx'), may hold values from -14 to 14
- values: bfloat16 [4, 32768, 1024], P('dp', 'ctx'), may hold values from -4.5 to 4.5
- cotangent: bfloat16 [4, 32768, 1024], P('dp', 'ctx'), may hold values from -6 to 6
- gain: float32 [1024], replicated, may hold values from 0.1 to 1.9
Outputs:
- attended: bfloat16 [4, 32768, 1024], P('dp', 'ctx')
- grad_queries: bfloat16 [4, 32768, 1024], P('dp', 'ctx')
- grad_keys: bfloat16 [4, 32768, 1024], P('dp', 'ctx')
- grad_values: bfloat16 [4, 32768, 1024], P('dp', 'ctx')
- gain_grad: float32 [1024], replicated
All inputs are finite; a program needn't handle non-finite values.
Results may differ from a plain program's by a relative error of at most 0.019.
The roundings to bfloat16 on the way count: a program that leaves them out, or rounds other values in their place, can miss the bound.
Values may be sent and summed in bfloat16 or wider, within the bound.
A program may use at most 192 MiB of HBM per device.

v0:
```python
import jax
import jax.numpy as jnp
from jax import lax
from jax.sharding import PartitionSpec as P

H = 8
HD = 128
BLOCK = 128
STRIDE = 1024
SUMMARY = 8


NEG = -1e30


def from_behind(value, axis, steps):
    count = lax.axis_size(axis)
    first, last = (max(0, -steps), min(count, count - steps))
    return lax.ppermute(value, axis, [(source, source + steps) for source in range(first, last)])


def to_rows(block_array):
    batch, blocks, heads, width = block_array.shape
    return block_array.transpose(0, 2, 1, 3).reshape(batch, heads, blocks * width)


def to_blocks(row_array, blocks):
    batch, heads, length = row_array.shape
    return row_array.reshape(batch, heads, blocks, length // blocks).transpose(0, 2, 1, 3)


def per_device(queries, keys, values, cotangent, gain):
    f32 = jnp.float32
    bf16 = jnp.bfloat16
    batch, length, width = queries.shape
    blocks = length // BLOCK
    segs = length // STRIDE
    own_sums = segs * SUMMARY
    ctx_count = lax.axis_size("ctx")
    rank = lax.axis_index("ctx")
    scale = HD ** (-0.5)
    scaled = (queries.astype(f32) * gain).astype(bf16)
    rim_keys, rim_values = from_behind(
        (keys[:, length - BLOCK :], values[:, length - BLOCK :]), "ctx", 1
    )
    own_sum_keys = keys.reshape(batch, segs, STRIDE, width)[:, :, STRIDE - SUMMARY :].reshape(
        batch, own_sums, width
    )
    own_sum_values = values.reshape(batch, segs, STRIDE, width)[:, :, STRIDE - SUMMARY :].reshape(
        batch, own_sums, width
    )
    sum_keys, sum_values = (
        lax.all_gather(own_sum_keys, "ctx", axis=1, tiled=True),
        lax.all_gather(own_sum_values, "ctx", axis=1, tiled=True),
    )
    total_sums = sum_keys.shape[1]
    sum_keys = sum_keys.reshape(batch, total_sums, H, HD)
    sum_values = sum_values.reshape(batch, total_sums, H, HD)
    ext_keys = jnp.concatenate([rim_keys, keys], 1).reshape(batch, blocks + 1, BLOCK, H, HD)
    ext_values = jnp.concatenate([rim_values, values], 1).reshape(batch, blocks + 1, BLOCK, H, HD)
    band_keys = jnp.concatenate([ext_keys[:, :-1], ext_keys[:, 1:]], 2)
    band_values = jnp.concatenate([ext_values[:, :-1], ext_values[:, 1:]], 2)
    query_blocks = scaled.reshape(batch, blocks, BLOCK, H, HD)
    scaled_rows = scaled.reshape(batch, length, H, HD)
    grad_rows = cotangent.reshape(batch, length, H, HD)
    grad_blocks = cotangent.reshape(batch, blocks, BLOCK, H, HD)
    query_index = jnp.arange(BLOCK, dtype=jnp.int32)[:, None]
    key_index = jnp.arange(2 * BLOCK, dtype=jnp.int32)[None, :]
    band = (key_index > query_index) & (key_index <= query_index + BLOCK)
    global_block = rank * blocks + jnp.arange(blocks, dtype=jnp.int32)
    band_mask = band[None] & ((global_block > 0)[:, None, None] | (key_index >= BLOCK)[None])
    band_mask = band_mask[None, :, None]
    slot = jnp.arange(total_sums, dtype=jnp.int32)
    sum_pos = slot // SUMMARY * STRIDE + STRIDE - SUMMARY + slot % SUMMARY
    query_pos = rank * length + jnp.arange(length, dtype=jnp.int32)
    sum_mask = (query_pos[:, None] - sum_pos[None, :] >= BLOCK)[None, None]
    band_scores = (
        jnp.einsum("bnqhd,bnkhd->bnhqk", query_blocks, band_keys, preferred_element_type=f32)
        * scale
    )
    band_scores = jnp.where(band_mask, band_scores, NEG)
    sum_scores = (
        jnp.einsum("bqhd,bshd->bhqs", scaled_rows, sum_keys, preferred_element_type=f32) * scale
    )
    sum_scores = jnp.where(sum_mask, sum_scores, NEG)
    top = jnp.maximum(to_rows(jnp.max(band_scores, -1)), jnp.max(sum_scores, -1))
    band_exp = jnp.where(band_mask, jnp.exp(band_scores - to_blocks(top, blocks)[..., None]), 0.0)
    sum_exp = jnp.where(sum_mask, jnp.exp(sum_scores - top[..., None]), 0.0)
    total = to_rows(jnp.sum(band_exp, -1)) + jnp.sum(sum_exp, -1)
    band_prob = band_exp / to_blocks(total, blocks)[..., None]
    sum_prob = sum_exp / total[..., None]
    band_prob_b = band_prob.astype(bf16)
    sum_prob_b = sum_prob.astype(bf16)
    mixed = jnp.einsum(
        "bnhqk,bnkhd->bnqhd", band_prob_b, band_values, preferred_element_type=f32
    ).reshape(batch, length, H, HD)
    mixed = mixed + jnp.einsum(
        "bhqs,bshd->bqhd", sum_prob_b, sum_values, preferred_element_type=f32
    )
    attended = mixed.reshape(batch, length, width).astype(bf16)
    delta = jnp.sum(
        grad_rows.astype(f32) * attended.reshape(batch, length, H, HD).astype(f32), -1
    ).transpose(0, 2, 1)
    band_dprob = jnp.einsum(
        "bnqhd,bnkhd->bnhqk", grad_blocks, band_values, preferred_element_type=f32
    )
    sum_dprob = jnp.einsum("bqhd,bshd->bhqs", grad_rows, sum_values, preferred_element_type=f32)
    band_ds = (band_prob * (band_dprob - to_blocks(delta, blocks)[..., None]) * scale).astype(bf16)
    sum_ds = (sum_prob * (sum_dprob - delta[..., None]) * scale).astype(bf16)
    band_dv = jnp.einsum("bnhqk,bnqhd->bnkhd", band_prob_b, grad_blocks, preferred_element_type=f32)
    band_dk = jnp.einsum("bnhqk,bnqhd->bnkhd", band_ds, query_blocks, preferred_element_type=f32)
    rim_dk, rim_dv = from_behind((band_dk[:, 0, :BLOCK], band_dv[:, 0, :BLOCK]), "ctx", -1)
    sum_dv = jnp.einsum(
        "bhqs,bqhd->bshd", sum_prob_b, grad_rows, preferred_element_type=f32
    ).reshape(batch, total_sums, width)
    sum_dk = jnp.einsum("bhqs,bqhd->bshd", sum_ds, scaled_rows, preferred_element_type=f32).reshape(
        batch, total_sums, width
    )
    whole_dk, whole_dv = lax.psum((sum_dk, sum_dv), "ctx")
    owned_dk = lax.dynamic_slice_in_dim(whole_dk, rank * own_sums, own_sums, 1)
    owned_dv = lax.dynamic_slice_in_dim(whole_dv, rank * own_sums, own_sums, 1)

    def fold_band(pairs, received, owned):
        later = jnp.concatenate([pairs[:, 1:, :BLOCK], received[:, None]], 1)
        folded = (pairs[:, :, BLOCK:] + later).reshape(batch, segs, STRIDE, width)
        folded = folded.at[:, :, STRIDE - SUMMARY :].add(owned.reshape(batch, segs, SUMMARY, width))
        return folded.reshape(batch, length, width).astype(bf16)

    grad_values = fold_band(band_dv, rim_dv, owned_dv)
    grad_keys = fold_band(band_dk, rim_dk, owned_dk)
    grad_scaled = jnp.einsum(
        "bnhqk,bnkhd->bnqhd", band_ds, band_keys, preferred_element_type=f32
    ).reshape(batch, length, H, HD)
    grad_scaled = grad_scaled + jnp.einsum(
        "bhqs,bshd->bqhd", sum_ds, sum_keys, preferred_element_type=f32
    )
    grad_scaled = grad_scaled.reshape(batch, length, width)
    grad_queries = (grad_scaled * gain).astype(bf16)
    gain_part = jnp.sum(grad_scaled * queries.astype(f32), (0, 1))
    gain_total = lax.psum(gain_part, ("dp", "ctx"))
    token_count = batch * lax.axis_size("dp") * length * ctx_count
    gain_grad = gain_total * token_count ** (-0.5)
    return (attended, grad_queries, grad_keys, grad_values, gain_grad)


def solution(mesh):
    in_specs = (
        P("dp", "ctx", None),
        P("dp", "ctx", None),
        P("dp", "ctx", None),
        P("dp", "ctx", None),
        P(),
    )
    out_specs = (
        P("dp", "ctx", None),
        P("dp", "ctx", None),
        P("dp", "ctx", None),
        P("dp", "ctx", None),
        P(),
    )
    return jax.shard_map(
        per_device, mesh=mesh, in_specs=in_specs, out_specs=out_specs, check_vma=False
    )
```

profile of v0, /device:TPU:8, one launch (start us, length us, event | category | flops | bytes accessed | tf_op | source)
XLA Modules:
  0.0 754.5 jit_solution(17129775396608550831)
XLA Ops:
  9.0 4.2 collective-permute-start
  14.9 4.8 collective-permute-start.1
  26.7 93.4 %all-gather = bf16[1,1,256,1024]{3,2,1,0:T(8,128)(2,1)S(1)} all-gather(bf16[1,1,8,1024]{3,2,1,0:T(8,128)(2,1)S(1)} %slice.118), channel_id=2, replica_groups=mesh['dp'=4,'ctx'=32] {'ctx'}, dimensions={2}, use_global_device_ids=true | all-gather | bytes 540672 | tf_op jit(solution)/shard_map/all_gather | solution.py:53
  120.3 95.3 %all-gather.1 = bf16[1,1,256,1024]{3,2,1,0:T(8,128)(2,1)} all-gather(bf16[1,1,8,1024]{3,2,1,0:T(8,128)(2,1)S(1)} %slice.121), channel_id=3, replica_groups=mesh['dp'=4,'ctx'=32] {'ctx'}, dimensions={2}, use_global_device_ids=true | all-gather | bytes 540672 | tf_op jit(solution)/shard_map/all_gather | solution.py:54
  219.8 6.6 fusion.3
  230.4 4.1 copy.86
  251.7 5.2 fusion.2
  256.9 5.7 fusion.5
  274.6 4.3 copy.81
  279.0 5.4 copy.84
  284.4 9.3 %convolution_bitcast_fusion = f32[1,8,256,8,128]{4,2,3,1,0:T(8,128)} fusion(bf16[8,128,8,128]{3,2,1,0:T(8,128)(2,1)} %bitcast.200, f32[8,8,128,256]{3,2,1,0:T(8,128)} %get-tuple-element.53, f32[8,8,128]{2,1,0:T(8,128)S(1)} %fusion.28, f32[8,8,128]{2,1,0:T(8,128)S(1)} %fusion.29, pred[8,128,256]{2,1,0:T(8,128)(4,1)S(1)} %broadcast_and_fusion), kind=kOutput, calls=%fused_computation.27 | convolution fusion | flops 549453824 | bytes 19202048 | tf_op jit(solution)/shard_map/bnhqk,bnqhd->bnkhd/dot_general | solution.py:110
  293.8 6.1 fusion.16
  300.0 7.2 multiply_reduce_fusion
  307.1 17.9 %fusion.1 = bf16[8,8,128,256]{3,2,1,0:T(8,128)(2,1)S(1)} fusion(f32[8,8,128]{2,1,0:T(8,128)} %bitcast.208, bf16[1,8,128,8,128]{4,2,3,1,0:T(8,128)(2,1)} %copy-done.17, bf16[1,8,128,8,128]{4,2,3,1,0:T(8,128)(2,1)} %copy-done.16, bf16[8,128,8,128]{3,2,1,0:T(8,128)(2,1)} %bitcast.201, f32[8,8,128]{2,1,0:T(8,128)} %copy-done.25, f32[8,8,128]{2,1,0:T(8,128)} %copy-done.21, ...), kind=kOutput, calls=%fused_computation.2 | convolution fusion | flops 564133888 | bytes 19234816 | tf_op jit(solution)/shard_map/bnqhd,bnkhd->bnhqk/dot_general | solution.py:104
  325.1 4.4 fusion.14
  329.5 4.4 copy.88
  333.9 5.5 copy.93
  339.4 8.1 %multiply_convert_fusion = bf16[8,1024,256]{1,2,0:T(8,128)(2,1)S(1)} fusion(f32[8,1024]{1,0:T(8,128)S(1)} %bitcast.209, bf16[1024,8,128]{0,2,1:T(8,128)(2,1)} %bitcast.198, bf16[256,8,128]{0,2,1:T(8,128)(2,1)} %bitcast.206, f32[8,1024]{1,0:T(8,128)S(1)} %copy-done.24, f32[8,1024]{1,0:T(8,128)S(1)} %copy-done.20, f32[8,1024,256]{1,2,0:T(8,128)} %get-tuple-element.55, ...), kind=kOutput, calls=%fused_computation.3 | convolution fusion | flops 555745280 | bytes 15564800 | tf_op jit(solution)/shard_map/bqhd,bshd->bhqs/dot_general | solution.py:107
  353.0 5.4 copy.94
  361.7 4.2 convolution_bitcast_fusion.1
  373.4 68.5 %psum.23 = f32[1024]{0:T(1024)S(1)} all-reduce(f32[1024]{0:T(1024)S(1)} %get-tuple-element.46), channel_id=1, replica_groups=mesh['dp'=4,'ctx'=32] {'dp','ctx'}, use_global_device_ids=true, to_apply=%region_8.9 | all-reduce | flops 1024 | bytes 8192 | tf_op jit(solution)/shard_map/psum | solution.py:140
  442.5 4.3 slice.123
  446.8 4.5 slice.127
  453.8 6.3 slice_add_fusion.1
  460.1 5.6 copy.96
  469.8 4.4 copy.103
  474.2 7.2 copy.138
  483.3 238.8 %all-reduce.3.cloned.1.call-done = (f32[1,256,1024]{1,2,0:T(8,128)}, f32[1,256,1024]{1,2,0:T(8,128)}) async-done(((f32[1,256,1024]{1,2,0:T(8,128)}, f32[1,256,1024]{1,2,0:T(8,128)}), (f32[1,256,1024]{1,2,0:T(8,128)}, f32[1,256,1024]{1,2,0:T(8,128)})) %all-reduce.3.cloned.1.call-update) | async-done | bytes 2097168 | tf_op jit(solution)/shard_map/psum | solution.py:119
  725.4 7.1 convert_element_type.88
  732.5 4.5 copy.111
  737.8 5.1 convert_element_type.87
  742.9 4.3 copy.110
  (134 shorter events, 77.4 us)
Async XLA Ops:
  7.2 16.1 %copy-start.22 = (f32[1024]{0:T(1024)S(1)}, f32[1024]{0:T(1024)}, u32[]{:S(2)}) copy-start(f32[1024]{0:T(1024)} %param.13) | copy-start | bytes 12292
  7.2 16.1 %copy-start.2 = (bf16[1,1024,1024]{2,1,0:T(8,128)(2,1)S(1)}, bf16[1,1024,1024]{2,1,0:T(8,128)(2,1)}, u32[]{:S(2)}) copy-start(bf16[1,1024,1024]{2,1,0:T(8,128)(2,1)} %param.9) | copy-start | bytes 6291460
  7.2 714.9 %all-reduce.3.cloned.1.call-start = ((), (), s32[]{:S(2)}) async-start(), calls=%async_computation | async-start | bytes 4194304 | tf_op jit(solution)/shard_map/psum | solution.py:119
  9.0 256.1 %collective-permute-start = (bf16[1,128,1024]{2,1,0:T(8,128)(2,1)}, bf16[1,128,1024]{2,1,0:T(8,128)(2,1)S(1)}, u32[]{:S(2)}, u32[]{:S(2)}) collective-permute-start(bf16[1,128,1024]{2,1,0:T(8,128)(2,1)} %slice.100), channel_id=1, source_target_pairs={{0,1},{1,2},{2,3},{3,4},{4,5},{5,6},{6,7},{7,8},{8,9},{9,10},{10,1... | collective-permute-start | bytes 786440 | tf_op jit(solution)/shard_map/ppermute | solution.py:19
  14.9 231.6 %collective-permute-start.1 = (bf16[1,128,1024]{2,1,0:T(8,128)(2,1)}, bf16[1,128,1024]{2,1,0:T(8,128)(2,1)}, u32[]{:S(2)}, u32[]{:S(2)}) collective-permute-start(bf16[1,128,1024]{2,1,0:T(8,128)(2,1)} %slice.103), channel_id=1, source_target_pairs={{0,1},{1,2},{2,3},{3,4},{4,5},{5,6},{6,7},{7,8},{8,9},{9,10},{10,1... | collective-permute-start | bytes 786440 | tf_op jit(solution)/shard_map/ppermute | solution.py:19
  250.7 6.2 copy-start.10
  250.7 12.0 %slice-start = ((s8[8388608]{0:T(1024)(128)(4,1)}), s8[4194304]{0:T(1024)(128)(4,1)S(1)}, s32[]{:S(2)}) async-start(s8[8388608]{0:T(1024)(128)(4,1)} %bitcast.171), calls=%async_computation.1 | async-start | bytes 8388608
  251.7 5.2 copy-start.12
  251.7 11.0 %slice-start.1 = ((s8[8388608]{0:T(1024)(128)(4,1)}), s8[4194304]{0:T(1024)(128)(4,1)S(1)}, s32[]{:S(2)}) async-start(s8[8388608]{0:T(1024)(128)(4,1)} %bitcast.171), calls=%async_computation.2 | async-start | bytes 8388608
  256.9 43.0 %copy-start.19 = (f32[8,1024]{1,0:T(8,128)}, f32[8,1024]{1,0:T(8,128)S(1)}, u32[]{:S(2)}) copy-start(f32[8,1024]{1,0:T(8,128)S(1)} %bitcast_maximum_fusion) | copy-start | bytes 98308
  256.9 27.5 %copy-start.21 = (f32[8,8,128]{2,1,0:T(8,128)}, f32[8,8,128]{2,1,0:T(8,128)S(1)}, u32[]{:S(2)}) copy-start(f32[8,8,128]{2,1,0:T(8,128)S(1)} %fusion.29) | copy-start | bytes 98308
  265.1 34.9 %copy-start.23 = (f32[8,1024]{1,0:T(8,128)}, f32[8,1024]{1,0:T(8,128)S(1)}, u32[]{:S(2)}) copy-start(f32[8,1024]{1,0:T(8,128)S(1)} %bitcast_add_fusion.2) | copy-start | bytes 98308
  265.1 19.3 %copy-start.25 = (f32[8,8,128]{2,1,0:T(8,128)}, f32[8,8,128]{2,1,0:T(8,128)S(1)}, u32[]{:S(2)}) copy-start(f32[8,8,128]{2,1,0:T(8,128)S(1)} %fusion.28) | copy-start | bytes 98308
  267.4 7.2 copy-start.16
  284.4 9.3 %copy-start.14 = (bf16[1,1024,1024]{1,2,0:T(8,128)(2,1)S(1)}, bf16[1,1024,1024]{1,2,0:T(8,128)(2,1)}, u32[]{:S(2)}) copy-start(bf16[1,1024,1024]{1,2,0:T(8,128)(2,1)} %copy.126) | copy-start | bytes 6291460
  284.4 15.5 %slice-start.2 = ((s8[8388608]{0:T(1024)(128)(4,1)}), s8[4194304]{0:T(1024)(128)(4,1)S(1)}, s32[]{:S(2)}) async-start(s8[8388608]{0:T(1024)(128)(4,1)} %bitcast.173), calls=%async_computation.3 | async-start | bytes 8388608
  293.8 6.2 slice-start.3
  293.8 6.2 copy-start.18
  293.8 13.4 %slice-start.6 = ((s8[8388608]{0:T(1024)(128)(4,1)}), s8[4194304]{0:T(1024)(128)(4,1)S(1)}, s32[]{:S(2)}) async-start(s8[8388608]{0:T(1024)(128)(4,1)} %bitcast.189), calls=%async_computation.7 | async-start | bytes 8388608
  300.0 7.2 slice-start.7
  307.1 17.9 %copy-start.11 = (bf16[1,8,128,8,128]{4,2,3,1,0:T(8,128)(2,1)S(1)}, bf16[1,8,128,8,128]{4,2,3,1,0:T(8,128)(2,1)}, u32[]{:S(2)}) copy-start(bf16[1,8,128,8,128]{4,2,3,1,0:T(8,128)(2,1)} %copy-done.10) | copy-start | bytes 6291460
  325.1 4.4 copy-start.1
  333.9 5.5 copy-start.20
  333.9 5.5 copy-start.24
  333.9 5.5 copy-start.26
  339.4 8.1 %copy-start.3 = (bf16[1,1024,1024]{1,2,0:T(8,128)(2,1)S(1)}, bf16[1,1024,1024]{1,2,0:T(8,128)(2,1)}, u32[]{:S(2)}) copy-start(bf16[1,1024,1024]{1,2,0:T(8,128)(2,1)} %copy.125) | copy-start | bytes 6291460
  360.4 105.3 %collective-permute-start.3 = (f32[1,128,8,128]{3,1,2,0:T(8,128)}, f32[1,128,8,128]{3,1,2,0:T(8,128)S(1)}, u32[]{:S(2)}, u32[]{:S(2)}) collective-permute-start(f32[1,128,8,128]{3,1,2,0:T(8,128)} %slice_bitcast_fusion), channel_id=1, source_target_pairs={{1,0},{2,1},{3,2},{4,3},{5,4},{6,5},{7,6},{8,7},{9,8},{10,9},{11,1... | collective-permute-start | bytes 1572872 | tf_op jit(solution)/shard_map/ppermute | solution.py:19
  361.7 9.6 %copy-start.6 = (f32[1,1024,1024]{2,1,0:T(8,128)S(1)}, f32[1,1024,1024]{2,1,0:T(8,128)}, u32[]{:S(2)}) copy-start(f32[1,1024,1024]{2,1,0:T(8,128)} %copy.94) | copy-start | bytes 12582916
  370.0 83.8 %collective-permute-start.2 = (f32[1,128,8,128]{1,3,2,0:T(8,128)}, f32[1,128,8,128]{1,3,2,0:T(8,128)S(1)}, u32[]{:S(2)}, u32[]{:S(2)}) collective-permute-start(f32[1,128,8,128]{1,3,2,0:T(8,128)} %slice_bitcast_fusion.1), channel_id=1, source_target_pairs={{1,0},{2,1},{3,2},{4,3},{5,4},{6,5},{7,6},{8,7},{9,8},{10,9},{11,1... | collective-permute-start | bytes 1572872 | tf_op jit(solution)/shard_map/ppermute | solution.py:19
  446.8 4.5 copy-start.15
  474.2 7.2 copy-start.4
  732.5 4.5 copy-start.7
  (8 other events, 23.9 us)
Sparse Core Ops, SparseCore 0:
  361.8 360.2 all-reduce.2
where the time goes:
time: 765 us; the launch traced here: 754 us
  blocking collectives  257 us (34%)
  waiting for transfers between devices  239 us (31%)
  local copies, waits for them, and re-layouts  109 us (14%)
  matrix products  78.5 us (10%)
  other arithmetic  44.2 us (6%)
  between operations  15 us (2%)
  starting transfers between devices  11.6 us (2%)
    psum x1, waiting for transfers between devices, per_device(): whole_dk, whole_dv = lax.psum((sum_dk, sum_dv), 'ctx')  239 us
    all_gather x1, blocking collectives, per_device(): lax.all_gather(own_sum_values, 'ctx', axis=1, tiled=True)  95.3 us
    all_gather x1, blocking collectives, per_device(): lax.all_gather(own_sum_keys, 'ctx', axis=1, tiled=True)  93.4 us
    psum x1, blocking collectives, per_device(): gain_total = lax.psum(gain_part, ('dp', 'ctx'))  68.5 us
    unnamed x83, local copies, waits for them, and re-layouts  36.2 us
    dot_general x1, matrix products, per_device(): jnp.einsum('bnqhd,bnkhd->bnhqk', grad_blocks, band_values, preferred_elem...  17.9 us
  transfers between devices with their start and end apart: 5, of which 1 were waited for; matrix products, arithmetic and copies ran while one was open for 14% of the time, Pallas kernels for 0%

commit v1 on v0

v1 whole, which is shorter than its diff:
```python
import functools

import jax
import jax.numpy as jnp
from jax import lax
from jax.experimental import pallas as pl
from jax.experimental.pallas import tpu as pltpu
from jax.sharding import PartitionSpec as P

f32 = jnp.float32
bf16 = jnp.bfloat16
MESH = pl.DeviceIdType.MESH

H = 8
HD = 128
BLOCK = 128
STRIDE = 1024
SUMMARY = 8
SCALE = HD**-0.5
LOG2E = 1.4426950408889634
NEG = -1e30
TILE = 256
PARTS = 2


def nt(a, b):
    return lax.dot_general(a, b, (((1,), (1,)), ((), ())), preferred_element_type=f32)


def nn(a, b):
    return lax.dot_general(a, b, (((1,), (0,)), ((), ())), preferred_element_type=f32)


def attend_head(rank, q_ref, do_ref, kx, vx, sk, sv, gain, o_ref, gq_ref, gk_ref, gv_ref):
    length = q_ref.shape[0]
    blocks = length // BLOCK
    nb = TILE // BLOCK
    slots = sk.shape[0]
    skT, svT, kxT, vxT = sk.T, sv.T, kx.T, vx.T
    before = lax.broadcasted_iota(jnp.int32, (BLOCK, BLOCK), 0) > lax.broadcasted_iota(
        jnp.int32, (BLOCK, BLOCK), 1
    )
    dk, dv = [None] * (blocks + 1), [None] * (blocks + 1)
    dsk = dsv = gp = None
    plus = lambda old, new: new if old is None else old + new
    none = jnp.zeros((BLOCK, BLOCK), bf16)

    for t in range(length // TILE):
        rows = pl.ds(t * TILE, TILE)
        first = t * nb
        near = slice(first * BLOCK, (first + nb + 1) * BLOCK)
        qf = q_ref[rows, :].astype(f32)
        qs = (qf * gain).astype(bf16)
        do = do_ref[rows, :]

        def band(full, start):
            columns = []
            for i in range(nb):
                lanes = slice(i * BLOCK, (i + 1) * BLOCK)
                earlier = full[i * BLOCK : (i + 1) * BLOCK, lanes]
                if start is not None and t == 0 and i == 0:
                    earlier = jnp.where(rank > 0, earlier, start)
                columns.append(jnp.where(before, earlier, full[(i + 1) * BLOCK : (i + 2) * BLOCK, lanes]))
            return jnp.concatenate(columns, 1)

        sb = band(nt(kx[near], qs), NEG)
        db = band(nt(vx[near], do), None)
        ss = nt(sk, qs)
        ds = nt(sv, do)
        slot = lax.broadcasted_iota(jnp.int32, (slots, TILE), 0)
        if t == 0:
            spos = slot // SUMMARY * STRIDE + STRIDE - SUMMARY + slot % SUMMARY
            qpos = rank * length + lax.broadcasted_iota(jnp.int32, (slots, TILE), 1)
            seen = qpos - spos >= BLOCK
        else:
            seen = slot < SUMMARY * rank
        ss = jnp.where(seen, ss, NEG)
        top = jnp.maximum(jnp.max(sb, 0, keepdims=True), jnp.max(ss, 0, keepdims=True))
        eb = jnp.exp2((sb - top) * (SCALE * LOG2E))
        es = jnp.exp2((ss - top) * (SCALE * LOG2E))
        inv = 1.0 / (jnp.sum(eb, 0, keepdims=True) + jnp.sum(es, 0, keepdims=True))
        pb, ps = eb * inv, es * inv
        delta = jnp.sum(pb * db, 0, keepdims=True) + jnp.sum(ps * ds, 0, keepdims=True)
        gb = pb * ((db - delta) * SCALE)
        gs = ps * ((ds - delta) * SCALE)

        def unfold(x, xs):
            strips = []
            for j in range(nb + 1):
                cells = []
                for i in range(nb):
                    cell = x[:, i * BLOCK : (i + 1) * BLOCK]
                    if j == i:
                        cells.append(jnp.where(before, cell, 0.0).astype(bf16))
                    elif j == i + 1:
                        cells.append(jnp.where(before, 0.0, cell).astype(bf16))
                    else:
                        cells.append(none)
                strips.append(jnp.concatenate(cells, 1))
            return jnp.concatenate(strips + [xs.astype(bf16)], 0)

        prob, dscore = unfold(pb, ps), unfold(gb, gs)
        dvt, dkt = nn(prob, do), nn(dscore, qs)
        for j in range(nb + 1):
            strip = slice(j * BLOCK, (j + 1) * BLOCK)
            dv[first + j] = plus(dv[first + j], dvt[strip])
            dk[first + j] = plus(dk[first + j], dkt[strip])
        dsv = plus(dsv, dvt[(nb + 1) * BLOCK :])
        dsk = plus(dsk, dkt[(nb + 1) * BLOCK :])
        o_ref[rows, :] = nn(jnp.concatenate([vxT[:, near], svT], 1), prob).T.astype(bf16)
        dq = nn(jnp.concatenate([kxT[:, near], skT], 1), dscore).T
        gq_ref[rows, :] = (dq * gain).astype(bf16)
        gp = plus(gp, jnp.sum(dq * qf, 0, keepdims=True))
        for j in range(nb):
            n = first + j
            if n > 0:
                gk_ref[pl.ds((n - 1) * BLOCK, BLOCK), :] = dk[n].astype(bf16)
                gv_ref[pl.ds((n - 1) * BLOCK, BLOCK), :] = dv[n].astype(bf16)
    return dk[0], dv[0], dk[blocks], dv[blocks], dsk, dsv, gp


def exchange_kernel(
    q_ref, do_ref, k_ref, v_ref, g_ref, k_all, v_all,
    o_ref, gq_ref, gk_out, gv_out, gain_out,
    rim, mine, sums, grim, rrim, gsum, rsum, gk, gv, tail, acc, gbuf, gsub, gall,
    rim_s, rim_r, sum_s, sum_r, grim_s, grim_r, gsum_s, gsum_r, ga_s, ga_r, gb_s, gb_r, loc, put,
):
    h = pl.program_id(0)
    dp, rank = lax.axis_index("dp"), lax.axis_index("ctx")
    dps, ranks = lax.axis_size("dp"), lax.axis_size("ctx")
    length = q_ref.shape[0]
    half = H // PARTS
    last = length - BLOCK
    pair, side = rank // 2, rank % 2
    cell, cells = dp * 2 + side, dps * 2
    pairs = ranks // 2

    def rim_copy(i, which):
        src = (k_all, v_all)[which].at[pl.ds(last, BLOCK), pl.ds(i * HD, HD)]
        return pltpu.make_async_remote_copy(
            src, rim.at[i, which], rim_s.at[i, which], rim_r.at[i, which],
            device_id={"ctx": jnp.minimum(rank + 1, ranks - 1)}, device_id_type=MESH,
        )

    def sum_copy(source, target):
        return pltpu.make_async_remote_copy(
            mine, sums.at[source], sum_s.at[target], sum_r.at[source],
            device_id={"ctx": target}, device_id_type=MESH,
        )

    def grim_copy(i):
        return pltpu.make_async_remote_copy(
            grim.at[i], rrim.at[i], grim_s.at[i], grim_r.at[i],
            device_id={"ctx": jnp.maximum(rank - 1, 0)}, device_id_type=MESH,
        )

    def gsum_copy(part, source, target):
        return pltpu.make_async_remote_copy(
            gsum.at[part, target], rsum.at[part, source], gsum_s.at[part, target], gsum_r.at[part, source],
            device_id={"ctx": target}, device_id_type=MESH,
        )

    def cell_copy(source, target):
        return pltpu.make_async_remote_copy(
            gbuf, gsub.at[source], ga_s.at[target], ga_r.at[source],
            device_id={"dp": target // 2, "ctx": pair * 2 + target % 2}, device_id_type=MESH,
        )

    def pair_copy(source, target):
        return pltpu.make_async_remote_copy(
            gsub.at[cell], gall.at[source], gb_s.at[target], gb_r.at[source],
            device_id={"ctx": target * 2 + side}, device_id_type=MESH,
        )

    def put_copy(i, which):
        lanes = pl.ds(pl.multiple_of(i * HD, HD), HD)
        out, held = ((gk_out, gk), (gv_out, gv))[which]
        return pltpu.make_async_copy(
            held.at[i % 2], out.at[pl.ds(0, last), lanes], put.at[i % 2, which]
        )

    def each(count, body, start=0):
        lax.fori_loop(start, count, lambda i, c: (body(i), c)[1], 0)

    @pl.when(h == 0)
    def _():
        own = [
            pltpu.make_async_copy(full.at[pl.ds(length - SUMMARY, SUMMARY), :], mine.at[i], loc.at[i])
            for i, full in enumerate((k_all, v_all))
        ]
        for copy in own:
            copy.start()
        barrier = pltpu.get_barrier_semaphore()

        def greet_rank(t):
            @pl.when(t != rank)
            def _():
                pl.semaphore_signal(barrier, inc=1, device_id={"ctx": t}, device_id_type=MESH)

        def greet_cell(c):
            @pl.when(c // 2 != dp)
            def _():
                pl.semaphore_signal(
                    barrier, inc=1, device_id={"dp": c // 2, "ctx": pair * 2 + c % 2}, device_id_type=MESH
                )

        each(ranks, greet_rank)
        each(cells, greet_cell)
        pl.semaphore_wait(barrier, ranks - 1 + cells - 2)

        @pl.when(rank < ranks - 1)
        def _():
            for which in range(2):
                rim_copy(0, which).start()

        for copy in own:
            copy.wait()
        each(ranks, lambda t: sum_copy(rank, t).start(), rank + 1)

        @pl.when(rank < ranks - 1)
        def _():
            for i in range(1, H):
                for which in range(2):
                    rim_copy(i, which).start()

        each(rank, lambda s: sum_copy(s, rank).wait_recv())

    @pl.when(rank > 0)
    def _():
        for which in range(2):
            rim_copy(h, which).wait_recv()

    @pl.when(h >= 2)
    def _():
        for which in range(2):
            put_copy(h - 2, which).wait()

    lanes = pl.ds(pl.multiple_of(h * HD, HD), HD)
    slots = sums.shape[0] * SUMMARY
    there = lax.broadcasted_iota(jnp.int32, (slots, HD), 0) < SUMMARY * rank

    def summary(which):
        rows = sums[:, which, :, lanes].astype(f32).reshape(slots, HD)
        return jnp.where(there, rows, 0.0).astype(bf16)

    def extended(which, ref):
        edge = jnp.where(rank > 0, rim[h, which], jnp.zeros((BLOCK, HD), bf16))
        return jnp.concatenate([edge, ref[...]], 0)

    dk0, dv0, dkn, dvn, dsk, dsv, gp = attend_head(
        rank, q_ref, do_ref, extended(0, k_ref), extended(1, v_ref), summary(0), summary(1), g_ref[...],
        o_ref, gq_ref, gk.at[h % 2], gv.at[h % 2],
    )
    for which in range(2):
        put_copy(h, which).start()
    grim[h, 0] = dk0.astype(bf16)
    grim[h, 1] = dv0.astype(bf16)
    tail[h, 0] = dkn
    tail[h, 1] = dvn
    part = h // half
    inner = pl.ds(pl.multiple_of(h % half * HD, HD), HD)
    gsum[part, :, 0, :, inner] = dsk.reshape(slots // SUMMARY, SUMMARY, HD).astype(bf16)
    gsum[part, :, 1, :, inner] = dsv.reshape(slots // SUMMARY, SUMMARY, HD).astype(bf16)
    gbuf[pl.ds(h, 1), :] = gp

    @pl.when(rank > 0)
    def _():
        grim_copy(h).start()

    @pl.when(h % half == half - 1)
    def _():
        each(rank, lambda t: gsum_copy(part, rank, t).start())

    @pl.when(h == H - 1)
    def _():
        def others(count, me, body):
            def one(i):
                @pl.when(i != me)
                def _():
                    body(i)

            each(count, one)

        others(cells, cell, lambda c: cell_copy(cell, c).start())
        others(cells, cell, lambda c: cell_copy(c, cell).wait_recv())
        others(cells, cell, lambda c: cell_copy(cell, c).wait_send())
        gsub[cell] = gbuf[...]
        total = gsub[0]
        for c in range(1, gsub.shape[0]):
            total = total + gsub[c]
        gsub[cell] = total
        gall[pair] = total
        others(pairs, pair, lambda p: pair_copy(pair, p).start())

        for p in range(PARTS):
            acc[p] = jnp.zeros(acc.shape[1:], f32)

        def collect(s):
            for p in range(PARTS):
                gsum_copy(p, s, rank).wait_recv()
                acc[p] = acc[p] + rsum[p, s].astype(f32)

        each(ranks, collect, rank + 1)

        @pl.when(rank < ranks - 1)
        def _():
            for i in range(H):
                grim_copy(i).wait_recv()
                for which in range(2):
                    tail[i, which] = tail[i, which] + rrim[i, which].astype(f32)

        for p in range(2):
            for which in range(2):
                put_copy(H - 2 + p, which).wait()
        for i in range(H):
            cols = slice((i % half) * HD, (i % half + 1) * HD)
            for which, held in enumerate((gk, gv)):
                cut = BLOCK - SUMMARY
                tail[i, which, cut:, :] = tail[i, which, cut:, :] + acc[i // half, which, :, cols]
                held[i // 7, pl.ds(i % 7 * BLOCK, BLOCK), :] = tail[i, which].astype(bf16)
        ends = [
            pltpu.make_async_copy(
                held.at[i // 7, pl.ds(i % 7 * BLOCK, BLOCK), :],
                out.at[pl.ds(last, BLOCK), pl.ds(i * HD, HD)],
                loc.at[2 + i * 2 + which],
            )
            for i in range(H)
            for which, (held, out) in enumerate(((gk, gk_out), (gv, gv_out)))
        ]
        for copy in ends:
            copy.start()

        others(pairs, pair, lambda p: pair_copy(p, pair).wait_recv())
        total = gall[0]
        for p in range(1, gall.shape[0]):
            total = total + gall[p]
        gain_out[...] = total * (dps * ranks * length) ** -0.5

        others(pairs, pair, lambda p: pair_copy(pair, p).wait_send())
        each(ranks, lambda t: sum_copy(rank, t).wait_send(), rank + 1)

        @pl.when(rank < ranks - 1)
        def _():
            for i in range(H):
                for which in range(2):
                    rim_copy(i, which).wait_send()

        @pl.when(rank > 0)
        def _():
            for i in range(H):
                grim_copy(i).wait_send()

        for p in range(PARTS):
            each(rank, lambda t, p=p: gsum_copy(p, rank, t).wait_send())
        for copy in ends:
            copy.wait()


def solution(mesh):
    dps, ranks = mesh.shape["dp"], mesh.shape["ctx"]

    def per_device(queries, keys, values, cotangent, gain):
        _, length, width = queries.shape
        flat = lambda x: x.reshape(length, width)
        q, k, v, do = flat(queries), flat(keys), flat(values), flat(cotangent)
        col = lambda rows: pl.BlockSpec((rows, HD), lambda h: (0, h))
        away = pl.BlockSpec(memory_space=pl.ANY)
        half = H // PARTS
        last = length - BLOCK
        big = jax.ShapeDtypeStruct((length, width), bf16)
        dma = lambda *shape: pltpu.SemaphoreType.DMA(shape)
        out = pl.pallas_call(
            exchange_kernel,
            name="attend_exchange",
            grid=(H,),
            in_specs=[col(length)] * 4 + [col(1), away, away],
            out_specs=[col(length), col(length), away, away, pl.BlockSpec((H, HD), lambda h: (0, 0))],
            out_shape=[big] * 4 + [jax.ShapeDtypeStruct((H, HD), f32)],
            scratch_shapes=[
                pltpu.VMEM((H, 2, BLOCK, HD), bf16),
                pltpu.VMEM((2, SUMMARY, width), bf16),
                pltpu.VMEM((ranks, 2, SUMMARY, width), bf16),
                pltpu.VMEM((H, 2, BLOCK, HD), bf16),
                pltpu.VMEM((H, 2, BLOCK, HD), bf16),
                pltpu.VMEM((PARTS, ranks, 2, SUMMARY, half * HD), bf16),
                pltpu.VMEM((PARTS, ranks, 2, SUMMARY, half * HD), bf16),
                pltpu.VMEM((2, last, HD), bf16),
                pltpu.VMEM((2, last, HD), bf16),
                pltpu.VMEM((H, 2, BLOCK, HD), f32),
                pltpu.VMEM((PARTS, 2, SUMMARY, half * HD), f32),
                pltpu.VMEM((H, HD), f32),
                pltpu.VMEM((dps * 2, H, HD), f32),
                pltpu.VMEM((ranks // 2, H, HD), f32),
                dma(H, 2), dma(H, 2),
                dma(ranks), dma(ranks),
                dma(H), dma(H),
                dma(PARTS, ranks), dma(PARTS, ranks),
                dma(dps * 2), dma(dps * 2),
                dma(ranks // 2), dma(ranks // 2),
                dma(2 + 2 * H), dma(2, 2),
            ],
            compiler_params=pltpu.CompilerParams(
                collective_id=0, has_side_effects=True, vmem_limit_bytes=48 << 20
            ),
        )(q, do, k, v, gain.reshape(1, width), k, v)
        whole = lambda x: x.reshape(1, length, width)
        return whole(out[0]), whole(out[1]), whole(out[2]), whole(out[3]), out[4].reshape(width)

    spread = P("dp", "ctx", None)
    return jax.shard_map(
        per_device,
        mesh=mesh,
        in_specs=(spread,) * 4 + (P(),),
        out_specs=(spread,) * 4 + (P(),),
        check_vma=False,
    )
```

time: 765 us -> 84.6 us (0.11)
  the two profiles are of different devices: /device:TPU:8 before, /device:TPU:1 now
where the time goes in v1:
time: 84.6 us; the launch traced here: 84.2 us
  Pallas kernels  75 us (89%)
  local copies, waits for them, and re-layouts  8.61 us (10%)
    pallas_call x1, Pallas kernels, per_device(): pl.pallas_call(exchange_kernel, name='attend_exchange', grid=(H,), in_spe...  75 us
    unnamed x11, local copies, waits for them, and re-layouts  8.61 us

profile of v1, /device:TPU:1, one launch (start us, length us, event | category | flops | bytes accessed | tf_op | source)
XLA Modules:
  0.0 84.2 jit_solution(9754718902077206717)
XLA Ops:
  0.6 0.0 copy-start
  0.6 0.7 copy-done
  1.3 75.0 %attend_exchange.1 = (bf16[1024,1024]{1,0:T(8,128)(2,1)S(1)}, bf16[1024,1024]{1,0:T(8,128)(2,1)S(1)}, bf16[1024,1024]{1,0:T(8,128)(2,1)}, bf16[1024,1024]{1,0:T(8,128)(2,1)}, f32[8,128]{1,0:T(8,128)S(1)}) custom-call(bf16[1024,1024]{1,0:T(8,128)(2,1)} %bitcast.20, bf16[1024,1024]{1,0:T(8,128)(2,1)} %bitcast.21, bf16[1024,1024]{1,0:T(8,128)(2,1)} %bitcast.14, ...), custom_call_target="tpu_custom_call" | custom-call | tf_op jit(solution)/shard_map/attend_exchange/pallas_call | solution.py:372
  76.3 1.3 %copy.15 = bf16[1,1024,1024]{2,1,0:T(8,128)(2,1)} copy(bf16[1,1024,1024]{2,1,0:T(8,128)(2,1)S(1)} %bitcast.11) | data formatting | bytes 4194304
  77.6 0.0 copy-start.2
  77.6 1.3 %copy.16 = bf16[1,1024,1024]{2,1,0:T(8,128)(2,1)} copy(bf16[1,1024,1024]{2,1,0:T(8,128)(2,1)S(1)} %bitcast.10) | data formatting | bytes 4194304
  78.9 1.0 %copy-done.2 = bf16[1024,1024]{1,0:T(8,128)(2,1)S(1)} copy-done((bf16[1024,1024]{1,0:T(8,128)(2,1)S(1)}, bf16[1024,1024]{1,0:T(8,128)(2,1)}, u32[]{:S(2)}) %copy-start.2) | copy-done | bytes 2097176
  80.0 0.0 copy-start.1
  80.0 1.3 %copy.17 = bf16[1,1024,1024]{2,1,0:T(8,128)(2,1)} copy(bf16[1,1024,1024]{2,1,0:T(8,128)(2,1)S(1)} %bitcast.19) | data formatting | bytes 4194304
  81.3 1.0 %copy-done.1 = bf16[1024,1024]{1,0:T(8,128)(2,1)S(1)} copy-done((bf16[1024,1024]{1,0:T(8,128)(2,1)S(1)}, bf16[1024,1024]{1,0:T(8,128)(2,1)}, u32[]{:S(2)}) %copy-start.1) | copy-done | bytes 2097176
  82.3 1.3 %copy.18 = bf16[1,1024,1024]{2,1,0:T(8,128)(2,1)} copy(bf16[1,1024,1024]{2,1,0:T(8,128)(2,1)S(1)} %bitcast.18) | data formatting | bytes 4194304
  83.6 0.6 copy.19
Async XLA Ops:
  0.6 0.7 copy-start
  77.6 2.3 %copy-start.2 = (bf16[1024,1024]{1,0:T(8,128)(2,1)S(1)}, bf16[1024,1024]{1,0:T(8,128)(2,1)}, u32[]{:S(2)}) copy-start(bf16[1024,1024]{1,0:T(8,128)(2,1)} %get-tuple-element.12) | copy-start | bytes 6291460
  80.0 2.3 %copy-start.1 = (bf16[1024,1024]{1,0:T(8,128)(2,1)S(1)}, bf16[1024,1024]{1,0:T(8,128)(2,1)}, u32[]{:S(2)}) copy-start(bf16[1024,1024]{1,0:T(8,128)(2,1)} %get-tuple-element.13) | copy-start | bytes 6291460

commit v2 on v1

--- a/solution.py
+++ b/solution.py
@@ -1,5 +1,3 @@
-import functools
-
 import jax
 import jax.numpy as jnp
 from jax import lax
@@ -20,7 +18,8 @@
 LOG2E = 1.4426950408889634
 NEG = -1e30
 TILE = 256
-PARTS = 2
+OUTWARD = (0, 1, 3, 8)
+BACK = (0, 5, 7, 8)
 
 
 def nt(a, b):
@@ -121,30 +120,34 @@
 
 def exchange_kernel(
     q_ref, do_ref, k_ref, v_ref, g_ref, k_all, v_all,
-    o_ref, gq_ref, gk_out, gv_out, gain_out,
-    rim, mine, sums, grim, rrim, gsum, rsum, gk, gv, tail, acc, gbuf, gsub, gall,
-    rim_s, rim_r, sum_s, sum_r, grim_s, grim_r, gsum_s, gsum_r, ga_s, ga_r, gb_s, gb_r, loc, put,
+    o_ref, gq_ref, gk_ref, gv_ref, ends_ref, gain_out,
+    rim, mine, sums, grim, rrim, gsum, rsum, tail, acc, gbuf, gsub, gall,
+    rim_s, rim_r, sum_s, sum_r, grim_s, grim_r, gsum_s, gsum_r, ga_s, ga_r, gb_s, gb_r, loc,
 ):
     h = pl.program_id(0)
     dp, rank = lax.axis_index("dp"), lax.axis_index("ctx")
     dps, ranks = lax.axis_size("dp"), lax.axis_size("ctx")
     length = q_ref.shape[0]
-    half = H // PARTS
     last = length - BLOCK
     pair, side = rank // 2, rank % 2
     cell, cells = dp * 2 + side, dps * 2
     pairs = ranks // 2
+    groups, parts = len(OUTWARD) - 1, len(BACK) - 1
+
+    def heads(edges, i):
+        return pl.ds(edges[i] * HD, (edges[i + 1] - edges[i]) * HD)
 
     def rim_copy(i, which):
-        src = (k_all, v_all)[which].at[pl.ds(last, BLOCK), pl.ds(i * HD, HD)]
+        src = (k_all, v_all)[which].at[pl.ds(last, BLOCK), pl.ds(pl.multiple_of(i * HD, HD), HD)]
         return pltpu.make_async_remote_copy(
             src, rim.at[i, which], rim_s.at[i, which], rim_r.at[i, which],
             device_id={"ctx": jnp.minimum(rank + 1, ranks - 1)}, device_id_type=MESH,
         )
 
-    def sum_copy(source, target):
-        return pltpu.make_async_remote_copy(
-            mine, sums.at[source], sum_s.at[target], sum_r.at[source],
+    def sum_copy(group, source, target):
+        lanes = heads(OUTWARD, group)
+        return pltpu.make_async_remote_copy(
+            mine.at[:, :, lanes], sums.at[source, :, :, lanes], sum_s.at[group, target], sum_r.at[group, source],
             device_id={"ctx": target}, device_id_type=MESH,
         )
 
@@ -155,8 +158,10 @@
         )
 
     def gsum_copy(part, source, target):
-        return pltpu.make_async_remote_copy(
-            gsum.at[part, target], rsum.at[part, source], gsum_s.at[part, target], gsum_r.at[part, source],
+        lanes = heads(BACK, part)
+        return pltpu.make_async_remote_copy(
+            gsum.at[target, :, :, lanes], rsum.at[source, :, :, lanes],
+            gsum_s.at[part, target], gsum_r.at[part, source],
             device_id={"ctx": target}, device_id_type=MESH,
         )
 
@@ -172,15 +177,17 @@
             device_id={"ctx": target * 2 + side}, device_id_type=MESH,
         )
 
-    def put_copy(i, which):
-        lanes = pl.ds(pl.multiple_of(i * HD, HD), HD)
-        out, held = ((gk_out, gk), (gv_out, gv))[which]
-        return pltpu.make_async_copy(
-            held.at[i % 2], out.at[pl.ds(0, last), lanes], put.at[i % 2, which]
-        )
-
     def each(count, body, start=0):
         lax.fori_loop(start, count, lambda i, c: (body(i), c)[1], 0)
+
+    def send_rim(i):
+        @pl.when(rank < ranks - 1)
+        def _():
+            for which in range(2):
+                rim_copy(i, which).start()
+
+    def send_sums(group):
+        each(ranks, lambda t: sum_copy(group, rank, t).start(), rank + 1)
 
     @pl.when(h == 0)
     def _():
@@ -206,34 +213,34 @@
 
         each(ranks, greet_rank)
         each(cells, greet_cell)
-        pl.semaphore_wait(barrier, ranks - 1 + cells - 2)
-
-        @pl.when(rank < ranks - 1)
-        def _():
-            for which in range(2):
-                rim_copy(0, which).start()
-
         for copy in own:
             copy.wait()
-        each(ranks, lambda t: sum_copy(rank, t).start(), rank + 1)
-
-        @pl.when(rank < ranks - 1)
-        def _():
-            for i in range(1, H):
-                for which in range(2):
-                    rim_copy(i, which).start()
-
-        each(rank, lambda s: sum_copy(s, rank).wait_recv())
+        pl.semaphore_wait(barrier, ranks - 1 + cells - 2)
+        send_rim(0)
+        send_sums(0)
+        send_rim(1)
+        send_sums(1)
+
+    @pl.when(h == 1)
+    def _():
+        send_rim(2)
+        for group in range(2, groups):
+            send_sums(group)
+
+    @pl.when((h >= 1) & (h + 2 < H))
+    def _():
+        send_rim(h + 2)
+
+    for group in range(groups):
+
+        @pl.when(h == OUTWARD[group])
+        def _(group=group):
+            each(rank, lambda s: sum_copy(group, s, rank).wait_recv())
 
     @pl.when(rank > 0)
     def _():
         for which in range(2):
             rim_copy(h, which).wait_recv()
-
-    @pl.when(h >= 2)
-    def _():
-        for which in range(2):
-            put_copy(h - 2, which).wait()
 
     lanes = pl.ds(pl.multiple_of(h * HD, HD), HD)
     slots = sums.shape[0] * SUMMARY
@@ -249,41 +256,36 @@
 
     dk0, dv0, dkn, dvn, dsk, dsv, gp = attend_head(
         rank, q_ref, do_ref, extended(0, k_ref), extended(1, v_ref), summary(0), summary(1), g_ref[...],
-        o_ref, gq_ref, gk.at[h % 2], gv.at[h % 2],
+        o_ref, gq_ref, gk_ref, gv_ref,
     )
-    for which in range(2):
-        put_copy(h, which).start()
     grim[h, 0] = dk0.astype(bf16)
     grim[h, 1] = dv0.astype(bf16)
     tail[h, 0] = dkn
     tail[h, 1] = dvn
-    part = h // half
-    inner = pl.ds(pl.multiple_of(h % half * HD, HD), HD)
-    gsum[part, :, 0, :, inner] = dsk.reshape(slots // SUMMARY, SUMMARY, HD).astype(bf16)
-    gsum[part, :, 1, :, inner] = dsv.reshape(slots // SUMMARY, SUMMARY, HD).astype(bf16)
+    gsum[:, 0, :, lanes] = dsk.reshape(slots // SUMMARY, SUMMARY, HD).astype(bf16)
+    gsum[:, 1, :, lanes] = dsv.reshape(slots // SUMMARY, SUMMARY, HD).astype(bf16)
     gbuf[pl.ds(h, 1), :] = gp
 
+    @pl.when(h == H - 1)
+    def _():
+        each(cells, lambda c: pl.when(c != cell)(lambda: cell_copy(cell, c).start()))
+
     @pl.when(rank > 0)
     def _():
         grim_copy(h).start()
 
-    @pl.when(h % half == half - 1)
-    def _():
-        each(rank, lambda t: gsum_copy(part, rank, t).start())
+    for part in range(parts):
+
+        @pl.when(h == BACK[part + 1] - 1)
+        def _(part=part):
+            each(rank, lambda t: gsum_copy(part, rank, t).start())
 
     @pl.when(h == H - 1)
     def _():
         def others(count, me, body):
-            def one(i):
-                @pl.when(i != me)
-                def _():
-                    body(i)
-
-            each(count, one)
-
-        others(cells, cell, lambda c: cell_copy(cell, c).start())
+            each(count, lambda i: pl.when(i != me)(lambda: body(i)))
+
         others(cells, cell, lambda c: cell_copy(c, cell).wait_recv())
-        others(cells, cell, lambda c: cell_copy(cell, c).wait_send())
         gsub[cell] = gbuf[...]
         total = gsub[0]
         for c in range(1, gsub.shape[0]):
@@ -292,13 +294,12 @@
         gall[pair] = total
         others(pairs, pair, lambda p: pair_copy(pair, p).start())
 
-        for p in range(PARTS):
-            acc[p] = jnp.zeros(acc.shape[1:], f32)
+        acc[...] = jnp.zeros(acc.shape, f32)
 
         def collect(s):
-            for p in range(PARTS):
-                gsum_copy(p, s, rank).wait_recv()
-                acc[p] = acc[p] + rsum[p, s].astype(f32)
+            for part in range(parts):
+                gsum_copy(part, s, rank).wait_recv()
+            acc[...] = acc[...] + rsum[s].astype(f32)
 
         each(ranks, collect, rank + 1)
 
@@ -309,26 +310,12 @@
                 for which in range(2):
                     tail[i, which] = tail[i, which] + rrim[i, which].astype(f32)
 
-        for p in range(2):
+        cut = BLOCK - SUMMARY
+        for i in range(H):
+            cols = slice(i * HD, (i + 1) * HD)
             for which in range(2):
-                put_copy(H - 2 + p, which).wait()
-        for i in range(H):
-            cols = slice((i % half) * HD, (i % half + 1) * HD)
-            for which, held in enumerate((gk, gv)):
-                cut = BLOCK - SUMMARY
-                tail[i, which, cut:, :] = tail[i, which, cut:, :] + acc[i // half, which, :, cols]
-                held[i // 7, pl.ds(i % 7 * BLOCK, BLOCK), :] = tail[i, which].astype(bf16)
-        ends = [
-            pltpu.make_async_copy(
-                held.at[i // 7, pl.ds(i % 7 * BLOCK, BLOCK), :],
-                out.at[pl.ds(last, BLOCK), pl.ds(i * HD, HD)],
-                loc.at[2 + i * 2 + which],
-            )
-            for i in range(H)
-            for which, (held, out) in enumerate(((gk, gk_out), (gv, gv_out)))
-        ]
-        for copy in ends:
-            copy.start()
+                tail[i, which, cut:, :] = tail[i, which, cut:, :] + acc[which, :, cols]
+                ends_ref[which, :, cols] = tail[i, which].astype(bf16)
 
         others(pairs, pair, lambda p: pair_copy(p, pair).wait_recv())
         total = gall[0]
@@ -336,8 +323,10 @@
             total = total + gall[p]
         gain_out[...] = total * (dps * ranks * length) ** -0.5
 
+        others(cells, cell, lambda c: cell_copy(cell, c).wait_send())
         others(pairs, pair, lambda p: pair_copy(pair, p).wait_send())
-        each(ranks, lambda t: sum_copy(rank, t).wait_send(), rank + 1)
+        for group in range(groups):
+            each(ranks, lambda t, group=group: sum_copy(group, rank, t).wait_send(), rank + 1)
 
         @pl.when(rank < ranks - 1)
         def _():
@@ -350,10 +339,30 @@
             for i in range(H):
                 grim_copy(i).wait_send()
 
-        for p in range(PARTS):
-            each(rank, lambda t, p=p: gsum_copy(p, rank, t).wait_send())
-        for copy in ends:
-            copy.wait()
+        for part in range(parts):
+            each(rank, lambda t, part=part: gsum_copy(part, rank, t).wait_send())
+
+
+def write_kernel(o_in, gq_in, gk_in, gv_in, ends_in, gain_in, o_out, gq_out, gk_out, gv_out, gain_out, sems):
+    last = gk_in.shape[0]
+    length = o_in.shape[0]
+    moves = []
+    for source, target in ((o_in, o_out), (gq_in, gq_out)):
+        for i in range(2):
+            rows = pl.ds(i * (length // 2), length // 2)
+            moves.append((source.at[rows], target.at[rows]))
+    for which, (source, target) in enumerate(((gk_in, gk_out), (gv_in, gv_out))):
+        for i in range(2):
+            rows = pl.ds(i * (last // 2), last // 2)
+            moves.append((source.at[rows], target.at[rows]))
+        moves.append((ends_in.at[which], target.at[pl.ds(last, length - last)]))
+    copies = [pltpu.make_async_copy(a, b, sems.at[i]) for i, (a, b) in enumerate(moves)]
+    for copy in copies:
+        copy.start()
+    for i in range(H):
+        gain_out[:, i * HD : (i + 1) * HD] = gain_in[i : i + 1, :]
+    for copy in copies:
+        copy.wait()
 
 
 def solution(mesh):
@@ -365,44 +374,56 @@
         q, k, v, do = flat(queries), flat(keys), flat(values), flat(cotangent)
         col = lambda rows: pl.BlockSpec((rows, HD), lambda h: (0, h))
         away = pl.BlockSpec(memory_space=pl.ANY)
-        half = H // PARTS
         last = length - BLOCK
-        big = jax.ShapeDtypeStruct((length, width), bf16)
+        like = jax.ShapeDtypeStruct
         dma = lambda *shape: pltpu.SemaphoreType.DMA(shape)
-        out = pl.pallas_call(
+        groups, parts = len(OUTWARD) - 1, len(BACK) - 1
+        held = pl.pallas_call(
             exchange_kernel,
             name="attend_exchange",
             grid=(H,),
             in_specs=[col(length)] * 4 + [col(1), away, away],
-            out_specs=[col(length), col(length), away, away, pl.BlockSpec((H, HD), lambda h: (0, 0))],
-            out_shape=[big] * 4 + [jax.ShapeDtypeStruct((H, HD), f32)],
+            out_specs=[col(length)] * 2
+            + [col(last)] * 2
+            + [pl.BlockSpec((2, BLOCK, width), lambda h: (0, 0, 0)), pl.BlockSpec((H, HD), lambda h: (0, 0))],
+            out_shape=[like((length, width), bf16)] * 2
+            + [like((last, width), bf16)] * 2
+            + [like((2, BLOCK, width), bf16), like((H, HD), f32)],
             scratch_shapes=[
                 pltpu.VMEM((H, 2, BLOCK, HD), bf16),
                 pltpu.VMEM((2, SUMMARY, width), bf16),
                 pltpu.VMEM((ranks, 2, SUMMARY, width), bf16),
                 pltpu.VMEM((H, 2, BLOCK, HD), bf16),
                 pltpu.VMEM((H, 2, BLOCK, HD), bf16),
-                pltpu.VMEM((PARTS, ranks, 2, SUMMARY, half * HD), bf16),
-                pltpu.VMEM((PARTS, ranks, 2, SUMMARY, half * HD), bf16),
-                pltpu.VMEM((2, last, HD), bf16),
-                pltpu.VMEM((2, last, HD), bf16),
+                pltpu.VMEM((ranks, 2, SUMMARY, width), bf16),
+                pltpu.VMEM((ranks, 2, SUMMARY, width), bf16),
                 pltpu.VMEM((H, 2, BLOCK, HD), f32),
-                pltpu.VMEM((PARTS, 2, SUMMARY, half * HD), f32),
+                pltpu.VMEM((2, SUMMARY, width), f32),
                 pltpu.VMEM((H, HD), f32),
                 pltpu.VMEM((dps * 2, H, HD), f32),
                 pltpu.VMEM((ranks // 2, H, HD), f32),
                 dma(H, 2), dma(H, 2),
-                dma(ranks), dma(ranks),
+                dma(groups, ranks), dma(groups, ranks),
                 dma(H), dma(H),
-                dma(PARTS, ranks), dma(PARTS, ranks),
+                dma(parts, ranks), dma(parts, ranks),
                 dma(dps * 2), dma(dps * 2),
                 dma(ranks // 2), dma(ranks // 2),
-                dma(2 + 2 * H), dma(2, 2),
+                dma(2),
             ],
             compiler_params=pltpu.CompilerParams(
-                collective_id=0, has_side_effects=True, vmem_limit_bytes=48 << 20
+                collective_id=0, has_side_effects=True, vmem_limit_bytes=44 << 20
             ),
         )(q, do, k, v, gain.reshape(1, width), k, v)
+        one = pl.BlockSpec(memory_space=pltpu.VMEM)
+        out = pl.pallas_call(
+            write_kernel,
+            name="attend_write",
+            in_specs=[away] * 5 + [one],
+            out_specs=[away] * 4 + [one],
+            out_shape=[like((length, width), bf16)] * 4 + [like((1, width), f32)],
+            scratch_shapes=[dma(10)],
+            compiler_params=pltpu.CompilerParams(vmem_limit_bytes=2 << 20),
+        )(*held)
         whole = lambda x: x.reshape(1, length, width)
         return whole(out[0]), whole(out[1]), whole(out[2]), whole(out[3]), out[4].reshape(width)
 

time: 84.6 us -> 79 us (0.934)
  local copies, waits for them, and re-layouts: 8.61 us -> 0.68 us
  Pallas kernels: 75 us -> 77.4 us
    unnamed x11 -> x2, local copies, waits for them, and re-layouts: 8.61 us -> 0.68 us
    pallas_call x0 -> x1, Pallas kernels: none -> 3.95 us  [per_device(): pl.pallas_call(write_kernel, name='attend_write', in_specs=[away] * 5 + [...]
    pallas_call x1, Pallas kernels: 75 us -> 73.5 us  [per_device(): pl.pallas_call(exchange_kernel, name='attend_exchange', grid=(H,), in_spe...]
where the time goes in v2:
time: 79 us; the launch traced here: 78.8 us
  Pallas kernels  77.4 us (98%)
    pallas_call x1, Pallas kernels, per_device(): pl.pallas_call(exchange_kernel, name='attend_exchange', grid=(H,), in_spe...  73.5 us
    pallas_call x1, Pallas kernels, per_device(): pl.pallas_call(write_kernel, name='attend_write', in_specs=[away] * 5 + [...  3.95 us

profile of v2, /device:TPU:1, one launch (start us, length us, event | category | flops | bytes accessed | tf_op | source)
XLA Modules:
  0.0 78.8 jit_solution(5596302383872672641)
XLA Ops:
  0.6 0.0 copy-start
  0.6 0.7 copy-done
  1.3 73.5 %attend_exchange.1 = (bf16[1024,1024]{1,0:T(8,128)(2,1)S(1)}, bf16[1024,1024]{1,0:T(8,128)(2,1)S(1)}, bf16[896,1024]{1,0:T(8,128)(2,1)S(1)}, bf16[896,1024]{1,0:...) custom-call(bf16[1024,1024]{1,0:T(8,128)(2,1)} %bitcast.15, bf16[1024,1024]{1,0:T(8,128)(2,1)} %bitcast.16, ...), custom_call_target="tpu_custom_call" | custom-call | tf_op jit(solution)/shard_map/attend_exchange/pallas_call | solution.py:381
  74.8 3.9 %attend_write.1 = (bf16[1024,1024]{1,0:T(8,128)(2,1)}, bf16[1024,1024]{1,0:T(8,128)(2,1)}, bf16[1024,1024]{1,0:T(8,128)(2,1)}, bf16[1024,1024]{1,0:T(8,128)(2,1)}, f32[1,1024]{1,0:T(1,128)}) custom-call(bf16[1024,1024]{1,0:T(8,128)(2,1)S(1)} %get-tuple-element.16.o_in, bf16[1024,1024]{1,0:T(8,128)(2,1)S(1)} %get-tuple-element.17.gq_in, ...), custom_call_target="tpu_custom_call" | custom-call | tf_op jit(solution)/shard_map/attend_write/pallas_call | solution.py:418
Async XLA Ops:
  0.6 0.7 copy-start

commit v3 on v2

--- a/solution.py
+++ b/solution.py
@@ -18,8 +18,9 @@
 LOG2E = 1.4426950408889634
 NEG = -1e30
 TILE = 256
-OUTWARD = (0, 1, 3, 8)
-BACK = (0, 5, 7, 8)
+OUTWARD = (0, 1, 3, 5, 8)
+BACK = (0, 2, 4, 6, 7, 8)
+EARLY = 3
 
 
 def nt(a, b):
@@ -121,8 +122,9 @@
 def exchange_kernel(
     q_ref, do_ref, k_ref, v_ref, g_ref, k_all, v_all,
     o_ref, gq_ref, gk_ref, gv_ref, ends_ref, gain_out,
-    rim, mine, sums, grim, rrim, gsum, rsum, tail, acc, gbuf, gsub, gall,
-    rim_s, rim_r, sum_s, sum_r, grim_s, grim_r, gsum_s, gsum_r, ga_s, ga_r, gb_s, gb_r, loc,
+    rim, sums, grim, rrim, gsum, rsum, tail, acc, racc, gbuf, gsub, gall,
+    rim_s, rim_r, part_s, part_r, sum_s, sum_r, grim_s, grim_r, gsum_s, gsum_r, gpart_s, gpart_r,
+    ga_s, ga_r, gb_s, gb_r, loc,
 ):
     h = pl.program_id(0)
     dp, rank = lax.axis_index("dp"), lax.axis_index("ctx")
@@ -130,12 +132,14 @@
     length = q_ref.shape[0]
     last = length - BLOCK
     pair, side = rank // 2, rank % 2
+    partner = pair * 2 + 1 - side
     cell, cells = dp * 2 + side, dps * 2
     pairs = ranks // 2
     groups, parts = len(OUTWARD) - 1, len(BACK) - 1
 
-    def heads(edges, i):
-        return pl.ds(edges[i] * HD, (edges[i + 1] - edges[i]) * HD)
+    def heads(edges, i, j=None):
+        j = i + 1 if j is None else j
+        return pl.ds(edges[i] * HD, (edges[j] - edges[i]) * HD)
 
     def rim_copy(i, which):
         src = (k_all, v_all)[which].at[pl.ds(last, BLOCK), pl.ds(pl.multiple_of(i * HD, HD), HD)]
@@ -144,11 +148,16 @@
             device_id={"ctx": jnp.minimum(rank + 1, ranks - 1)}, device_id_type=MESH,
         )
 
+    def part_copy(source):
+        return pltpu.make_async_remote_copy(
+            sums.at[source], sums.at[source], part_s, part_r, device_id={"ctx": partner}, device_id_type=MESH
+        )
+
     def sum_copy(group, source, target):
-        lanes = heads(OUTWARD, group)
-        return pltpu.make_async_remote_copy(
-            mine.at[:, :, lanes], sums.at[source, :, :, lanes], sum_s.at[group, target], sum_r.at[group, source],
-            device_id={"ctx": target}, device_id_type=MESH,
+        both, lanes = pl.ds(source * 2, 2), heads(OUTWARD, group)
+        return pltpu.make_async_remote_copy(
+            sums.at[both, :, :, lanes], sums.at[both, :, :, lanes], sum_s.at[group, target], sum_r.at[group, source],
+            device_id={"ctx": target * 2 + side}, device_id_type=MESH,
         )
 
     def grim_copy(i):
@@ -160,9 +169,16 @@
     def gsum_copy(part, source, target):
         lanes = heads(BACK, part)
         return pltpu.make_async_remote_copy(
-            gsum.at[target, :, :, lanes], rsum.at[source, :, :, lanes],
+            gsum.at[pl.ds(target * 2, 2), :, :, lanes], rsum.at[source, :, :, :, lanes],
             gsum_s.at[part, target], gsum_r.at[part, source],
-            device_id={"ctx": target}, device_id_type=MESH,
+            device_id={"ctx": target * 2 + side}, device_id_type=MESH,
+        )
+
+    def gpart_copy(late):
+        lanes = heads(BACK, EARLY, parts) if late else heads(BACK, 0, EARLY)
+        return pltpu.make_async_remote_copy(
+            acc.at[1 - side, :, :, lanes], racc.at[:, :, lanes], gpart_s.at[late], gpart_r.at[late],
+            device_id={"ctx": partner}, device_id_type=MESH,
         )
 
     def cell_copy(source, target):
@@ -179,6 +195,9 @@
 
     def each(count, body, start=0):
         lax.fori_loop(start, count, lambda i, c: (body(i), c)[1], 0)
+
+    def others(count, me, body):
+        each(count, lambda i: pl.when(i != me)(lambda: body(i)))
 
     def send_rim(i):
         @pl.when(rank < ranks - 1)
@@ -187,39 +206,61 @@
                 rim_copy(i, which).start()
 
     def send_sums(group):
-        each(ranks, lambda t: sum_copy(group, rank, t).start(), rank + 1)
+        each(pairs, lambda t: sum_copy(group, pair, t).start(), pair + 1)
+
+    def collect(some, lanes):
+        acc[:, :, :, lanes] = gsum[pl.ds(pair * 2, 2), :, :, lanes].astype(f32)
+
+        def add(s):
+            for part in some:
+                gsum_copy(part, s, pair).wait_recv()
+            acc[:, :, :, lanes] = acc[:, :, :, lanes] + rsum[s, :, :, :, lanes].astype(f32)
+
+        each(pairs, add, pair + 1)
+
+    def close(i):
+        @pl.when(rank < ranks - 1)
+        def _():
+            grim_copy(i).wait_recv()
+            for which in range(2):
+                tail[i, which] = tail[i, which] + rrim[i, which].astype(f32)
+
+        for which in range(2):
+            ends_ref[which, :, i * HD : (i + 1) * HD] = tail[i, which].astype(bf16)
 
     @pl.when(h == 0)
     def _():
         own = [
-            pltpu.make_async_copy(full.at[pl.ds(length - SUMMARY, SUMMARY), :], mine.at[i], loc.at[i])
+            pltpu.make_async_copy(
+                full.at[pl.ds(length - SUMMARY, SUMMARY), :], sums.at[rank, i], loc.at[i]
+            )
             for i, full in enumerate((k_all, v_all))
         ]
         for copy in own:
             copy.start()
         barrier = pltpu.get_barrier_semaphore()
 
-        def greet_rank(t):
-            @pl.when(t != rank)
-            def _():
-                pl.semaphore_signal(barrier, inc=1, device_id={"ctx": t}, device_id_type=MESH)
-
-        def greet_cell(c):
-            @pl.when(c // 2 != dp)
-            def _():
-                pl.semaphore_signal(
-                    barrier, inc=1, device_id={"dp": c // 2, "ctx": pair * 2 + c % 2}, device_id_type=MESH
-                )
-
-        each(ranks, greet_rank)
-        each(cells, greet_cell)
+        def greet(**device):
+            pl.semaphore_signal(barrier, inc=1, device_id=device, device_id_type=MESH)
+
+        others(pairs, pair, lambda p: greet(ctx=p * 2 + side))
+        others(cells, cell, lambda c: greet(dp=c // 2, ctx=pair * 2 + c % 2))
+        beside = rank + 2 * side - 1
+        inside = (beside >= 0) & (beside < ranks)
+
+        @pl.when(inside)
+        def _():
+            greet(ctx=jnp.clip(beside, 0, ranks - 1))
+
         for copy in own:
             copy.wait()
-        pl.semaphore_wait(barrier, ranks - 1 + cells - 2)
+        pl.semaphore_wait(barrier, pairs - 1 + cells - 1 + inside.astype(jnp.int32))
+        part_copy(rank).start()
         send_rim(0)
+        part_copy(partner).wait_recv()
         send_sums(0)
+        send_sums(1)
         send_rim(1)
-        send_sums(1)
 
     @pl.when(h == 1)
     def _():
@@ -235,7 +276,7 @@
 
         @pl.when(h == OUTWARD[group])
         def _(group=group):
-            each(rank, lambda s: sum_copy(group, s, rank).wait_recv())
+            each(pair, lambda s: sum_copy(group, s, pair).wait_recv())
 
     @pl.when(rank > 0)
     def _():
@@ -266,25 +307,39 @@
     gsum[:, 1, :, lanes] = dsv.reshape(slots // SUMMARY, SUMMARY, HD).astype(bf16)
     gbuf[pl.ds(h, 1), :] = gp
 
+    @pl.when(rank > 0)
+    def _():
+        grim_copy(h).start()
+
     @pl.when(h == H - 1)
     def _():
-        each(cells, lambda c: pl.when(c != cell)(lambda: cell_copy(cell, c).start()))
-
-    @pl.when(rank > 0)
-    def _():
-        grim_copy(h).start()
+        others(cells, cell, lambda c: cell_copy(cell, c).start())
 
     for part in range(parts):
 
         @pl.when(h == BACK[part + 1] - 1)
         def _(part=part):
-            each(rank, lambda t: gsum_copy(part, rank, t).start())
+            each(pair, lambda t: gsum_copy(part, pair, t).start())
+
+    @pl.when(h == H - 2)
+    def _():
+        for group in range(groups):
+            each(pairs, lambda t, group=group: sum_copy(group, pair, t).wait_send(), pair + 1)
+        part_copy(rank).wait_send()
+
+        @pl.when(rank < ranks - 1)
+        def _():
+            for i in range(H):
+                for which in range(2):
+                    rim_copy(i, which).wait_send()
+
+        for i in range(H - 3):
+            close(i)
 
     @pl.when(h == H - 1)
     def _():
-        def others(count, me, body):
-            each(count, lambda i: pl.when(i != me)(lambda: body(i)))
-
+        collect(range(EARLY), heads(BACK, 0, EARLY))
+        gpart_copy(0).start()
         others(cells, cell, lambda c: cell_copy(c, cell).wait_recv())
         gsub[cell] = gbuf[...]
         total = gsub[0]
@@ -293,29 +348,19 @@
         gsub[cell] = total
         gall[pair] = total
         others(pairs, pair, lambda p: pair_copy(pair, p).start())
-
-        acc[...] = jnp.zeros(acc.shape, f32)
-
-        def collect(s):
-            for part in range(parts):
-                gsum_copy(part, s, rank).wait_recv()
-            acc[...] = acc[...] + rsum[s].astype(f32)
-
-        each(ranks, collect, rank + 1)
-
-        @pl.when(rank < ranks - 1)
-        def _():
-            for i in range(H):
-                grim_copy(i).wait_recv()
-                for which in range(2):
-                    tail[i, which] = tail[i, which] + rrim[i, which].astype(f32)
-
-        cut = BLOCK - SUMMARY
+        collect(range(EARLY, parts), heads(BACK, EARLY, parts))
+        gpart_copy(1).start()
+        for i in range(H - 3, H):
+            close(i)
+        for late in range(2):
+            gpart_copy(late).wait_recv()
         for i in range(H):
             cols = slice(i * HD, (i + 1) * HD)
             for which in range(2):
-                tail[i, which, cut:, :] = tail[i, which, cut:, :] + acc[which, :, cols]
-                ends_ref[which, :, cols] = tail[i, which].astype(bf16)
+                extra = acc[side, which, :, cols] + racc[which, :, cols]
+                ends_ref[which, BLOCK - 16 :, cols] = (
+                    tail[i, which, BLOCK - 16 :, :] + jnp.concatenate([jnp.zeros((16 - SUMMARY, HD), f32), extra], 0)
+                ).astype(bf16)
 
         others(pairs, pair, lambda p: pair_copy(p, pair).wait_recv())
         total = gall[0]
@@ -325,14 +370,6 @@
 
         others(cells, cell, lambda c: cell_copy(cell, c).wait_send())
         others(pairs, pair, lambda p: pair_copy(pair, p).wait_send())
-        for group in range(groups):
-            each(ranks, lambda t, group=group: sum_copy(group, rank, t).wait_send(), rank + 1)
-
-        @pl.when(rank < ranks - 1)
-        def _():
-            for i in range(H):
-                for which in range(2):
-                    rim_copy(i, which).wait_send()
 
         @pl.when(rank > 0)
         def _():
@@ -340,7 +377,9 @@
                 grim_copy(i).wait_send()
 
         for part in range(parts):
-            each(rank, lambda t, part=part: gsum_copy(part, rank, t).wait_send())
+            each(pair, lambda t, part=part: gsum_copy(part, pair, t).wait_send())
+        for late in range(2):
+            gpart_copy(late).wait_send()
 
 
 def write_kernel(o_in, gq_in, gk_in, gv_in, ends_in, gain_in, o_out, gq_out, gk_out, gv_out, gain_out, sems):
@@ -391,21 +430,23 @@
             + [like((2, BLOCK, width), bf16), like((H, HD), f32)],
             scratch_shapes=[
                 pltpu.VMEM((H, 2, BLOCK, HD), bf16),
-                pltpu.VMEM((2, SUMMARY, width), bf16),
                 pltpu.VMEM((ranks, 2, SUMMARY, width), bf16),
                 pltpu.VMEM((H, 2, BLOCK, HD), bf16),
                 pltpu.VMEM((H, 2, BLOCK, HD), bf16),
                 pltpu.VMEM((ranks, 2, SUMMARY, width), bf16),
-                pltpu.VMEM((ranks, 2, SUMMARY, width), bf16),
+                pltpu.VMEM((ranks // 2, 2, 2, SUMMARY, width), bf16),
                 pltpu.VMEM((H, 2, BLOCK, HD), f32),
+                pltpu.VMEM((2, 2, SUMMARY, width), f32),
                 pltpu.VMEM((2, SUMMARY, width), f32),
                 pltpu.VMEM((H, HD), f32),
                 pltpu.VMEM((dps * 2, H, HD), f32),
                 pltpu.VMEM((ranks // 2, H, HD), f32),
                 dma(H, 2), dma(H, 2),
-                dma(groups, ranks), dma(groups, ranks),
+                pltpu.SemaphoreType.DMA, pltpu.SemaphoreType.DMA,
+                dma(groups, ranks // 2), dma(groups, ranks // 2),
                 dma(H), dma(H),
-                dma(parts, ranks), dma(parts, ranks),
+                dma(parts, ranks // 2), dma(parts, ranks // 2),
+                dma(2), dma(2),
                 dma(dps * 2), dma(dps * 2),
                 dma(ranks // 2), dma(ranks // 2),
                 dma(2),

time: 79 us -> 67.6 us (0.86)
  Pallas kernels: 77.4 us -> 66 us
    pallas_call x1, Pallas kernels: 73.5 us -> 62.1 us  [per_device(): pl.pallas_call(exchange_kernel, name='attend_exchange', grid=(H,), in_spe...]
where the time goes in v3:
time: 67.6 us; the launch traced here: 67.3 us
  Pallas kernels  66 us (98%)
  local copies, waits for them, and re-layouts  0.68 us (1%)
    pallas_call x1, Pallas kernels, per_device(): pl.pallas_call(exchange_kernel, name='attend_exchange', grid=(H,), in_spe...  62.1 us
    pallas_call x1, Pallas kernels, per_device(): pl.pallas_call(write_kernel, name='attend_write', in_specs=[away] * 5 + [...  3.95 us

profile of v3, /device:TPU:1, one launch (start us, length us, event | category | flops | bytes accessed | tf_op | source)
XLA Modules:
  0.0 67.3 jit_solution(3319435215944883604)
XLA Ops:
  0.6 0.0 copy-start
  0.6 0.7 %copy-done = f32[1024]{0:T(1024)S(1)} copy-done((f32[1024]{0:T(1024)S(1)}, f32[1024]{0:T(1024)}, u32[]{:S(2)}) %copy-start) | copy-done | bytes 4120
  1.3 62.1 %attend_exchange.1 = (bf16[1024,1024]{1,0:T(8,128)(2,1)S(1)}, bf16[1024,1024]{1,0:T(8,128)(2,1)S(1)}, bf16[896,1024]{1,0:T(8,128)(2,1)S(1)}, bf16[896,1024]{1,0:...) custom-call(bf16[1024,1024]{1,0:T(8,128)(2,1)} %bitcast.15, bf16[1024,1024]{1,0:T(8,128)(2,1)} %bitcast.16, ...), custom_call_target="tpu_custom_call" | custom-call | tf_op jit(solution)/shard_map/attend_exchange/pallas_call | solution.py:420
  63.4 3.9 %attend_write.1 = (bf16[1024,1024]{1,0:T(8,128)(2,1)}, bf16[1024,1024]{1,0:T(8,128)(2,1)}, bf16[1024,1024]{1,0:T(8,128)(2,1)}, bf16[1024,1024]{1,0:T(8,128)(2,1)}, f32[1,1024]{1,0:T(1,128)}) custom-call(bf16[1024,1024]{1,0:T(8,128)(2,1)S(1)} %get-tuple-element.16.o_in, bf16[1024,1024]{1,0:T(8,128)(2,1)S(1)} %get-tuple-element.17.gq_in, ...), custom_call_target="tpu_custom_call" | custom-call | tf_op jit(solution)/shard_map/attend_write/pallas_call | solution.py:459
Async XLA Ops:
  0.6 0.7 %copy-start = (f32[1024]{0:T(1024)S(1)}, f32[1024]{0:T(1024)}, u32[]{:S(2)}) copy-start(f32[1024]{0:T(1024)} %param.9) | copy-start | bytes 12292

commit v4 on v3

v4 whole, which is shorter than its diff:
```python
import jax
import jax.numpy as jnp
from jax import lax
from jax.experimental import pallas as pl
from jax.experimental.pallas import tpu as pltpu
from jax.sharding import PartitionSpec as P

f32 = jnp.float32
bf16 = jnp.bfloat16
MESH = pl.DeviceIdType.MESH

H = 8
HD = 128
BLOCK = 128
STRIDE = 1024
SUMMARY = 8
SCALE = HD**-0.5
LOG2E = 1.4426950408889634
NEG = -1e30
TILE = 256
OUTWARD = (0, 1, 3, 8)
BACK = (0, 3, 6, 8)
EARLY = 2
AHEAD = 4


def nt(a, b):
    return lax.dot_general(a, b, (((1,), (1,)), ((), ())), preferred_element_type=f32)


def nn(a, b):
    return lax.dot_general(a, b, (((1,), (0,)), ((), ())), preferred_element_type=f32)


def plus(old, new):
    return new if old is None else old + new


def exchange_kernel(
    q_all, do_all, k_all, v_all, g_all,
    o_ref, gq_ref, gk_ref, gv_ref, gain_out,
    q, do, qs, kx, vx, g, sb, db, pst, gst, sums, grim, rrim, gsum, rsum, edge, acc, racc, gbuf, gsub, gall,
    rim_s, rim_r, part_s, part_r, sum_s, sum_r, grim_s, grim_r, gsum_s, gsum_r, gpart_s, gpart_r,
    ga_s, ga_r, gb_s, gb_r, loc, load,
):
    dp, rank = lax.axis_index("dp"), lax.axis_index("ctx")
    dps, ranks = lax.axis_size("dp"), lax.axis_size("ctx")
    length = q.shape[1]
    blocks = length // BLOCK
    last = length - BLOCK
    pair, side = rank // 2, rank % 2
    partner = pair * 2 + 1 - side
    cell, cells = dp * 2 + side, dps * 2
    pairs = ranks // 2
    groups, parts = len(OUTWARD) - 1, len(BACK) - 1

    def heads(edges, i, j=None):
        j = i + 1 if j is None else j
        return pl.ds(edges[i] * HD, (edges[j] - edges[i]) * HD)

    def rim_copy(i, which):
        src = (k_all, v_all)[which].at[pl.ds(last, BLOCK), pl.ds(pl.multiple_of(i * HD, HD), HD)]
        return pltpu.make_async_remote_copy(
            src, (kx, vx)[which].at[i, pl.ds(0, BLOCK), :], rim_s.at[i, which], rim_r.at[i, which],
            device_id={"ctx": jnp.minimum(rank + 1, ranks - 1)}, device_id_type=MESH,
        )

    def part_copy(source):
        return pltpu.make_async_remote_copy(
            sums.at[source], sums.at[source], part_s, part_r, device_id={"ctx": partner}, device_id_type=MESH
        )

    def sum_copy(group, source, target):
        both, lanes = pl.ds(source * 2, 2), heads(OUTWARD, group)
        return pltpu.make_async_remote_copy(
            sums.at[both, :, :, lanes], sums.at[both, :, :, lanes], sum_s.at[group, target], sum_r.at[group, source],
            device_id={"ctx": target * 2 + side}, device_id_type=MESH,
        )

    def grim_copy(i):
        return pltpu.make_async_remote_copy(
            grim.at[i], rrim.at[i], grim_s.at[i], grim_r.at[i],
            device_id={"ctx": jnp.maximum(rank - 1, 0)}, device_id_type=MESH,
        )

    def gsum_copy(part, source, target):
        lanes = heads(BACK, part)
        return pltpu.make_async_remote_copy(
            gsum.at[pl.ds(target * 2, 2), :, :, lanes], rsum.at[source, :, :, :, lanes],
            gsum_s.at[part, target], gsum_r.at[part, source],
            device_id={"ctx": target * 2 + side}, device_id_type=MESH,
        )

    def gpart_copy(late):
        lanes = heads(BACK, EARLY, parts) if late else heads(BACK, 0, EARLY)
        return pltpu.make_async_remote_copy(
            acc.at[1 - side, :, :, lanes], racc.at[:, :, lanes], gpart_s.at[late], gpart_r.at[late],
            device_id={"ctx": partner}, device_id_type=MESH,
        )

    def cell_copy(source, target):
        return pltpu.make_async_remote_copy(
            gbuf, gsub.at[source], ga_s.at[target], ga_r.at[source],
            device_id={"dp": target // 2, "ctx": pair * 2 + target % 2}, device_id_type=MESH,
        )

    def pair_copy(source, target):
        return pltpu.make_async_remote_copy(
            gsub.at[cell], gall.at[source], gb_s.at[target], gb_r.at[source],
            device_id={"ctx": target * 2 + side}, device_id_type=MESH,
        )

    def each(count, body, start=0):
        lax.fori_loop(start, count, lambda i, c: (body(i), c)[1], 0)

    def others(count, me, body):
        each(count, lambda i: pl.when(i != me)(lambda: body(i)))

    def send_rim(i):
        @pl.when(rank < ranks - 1)
        def _():
            for which in range(2):
                rim_copy(i, which).start()

    def send_sums(group):
        each(pairs, lambda t: sum_copy(group, pair, t).start(), pair + 1)

    def collect(some, lanes):
        acc[:, :, :, lanes] = gsum[pl.ds(pair * 2, 2), :, :, lanes].astype(f32)

        def add(s):
            for part in some:
                gsum_copy(part, s, pair).wait_recv()
            acc[:, :, :, lanes] = acc[:, :, :, lanes] + rsum[s, :, :, :, lanes].astype(f32)

        each(pairs, add, pair + 1)

    def load_copy(i, which):
        source, target = ((q_all, q), (do_all, do), (k_all, kx), (v_all, vx))[which]
        rows = pl.ds(BLOCK, length) if which >= 2 else pl.ds(0, length)
        lanes = pl.ds(pl.multiple_of(i * HD, HD), HD)
        return pltpu.make_async_copy(source.at[:, lanes], target.at[i, rows, :], load.at[i, which])

    nb = TILE // BLOCK
    slots = sums.shape[0] * SUMMARY
    before = lax.broadcasted_iota(jnp.int32, (BLOCK, BLOCK), 0) > lax.broadcasted_iota(
        jnp.int32, (BLOCK, BLOCK), 1
    )
    wide = lax.broadcasted_iota(jnp.int32, (BLOCK, TILE), 0) > (
        lax.broadcasted_iota(jnp.int32, (BLOCK, TILE), 1) & (BLOCK - 1)
    )
    there = lax.broadcasted_iota(jnp.int32, (slots, HD), 0) < SUMMARY * rank
    none = jnp.zeros((BLOCK, BLOCK), bf16)

    def cols(h):
        return pl.ds(pl.multiple_of(h * HD, HD), HD)

    def summary(h, which):
        rows = sums[:, which, :, cols(h)].astype(f32).reshape(slots, HD)
        return jnp.where(there, rows, 0.0).astype(bf16)

    def banded(h):
        for i in range(4):
            load_copy(h, i).wait()
        gain = g[:, cols(h)]
        for t in range(length // TILE):
            rows = pl.ds(t * TILE, TILE)
            scaled = (q[h, rows, :].astype(f32) * gain).astype(bf16)
            qs[h, rows, :] = scaled
            skip = 1 if t == 0 else 0
            near = pl.ds((t * nb + skip) * BLOCK, (nb + 1 - skip) * BLOCK)
            for held, ext, other in ((sb, kx, scaled), (db, vx, do[h, rows, :])):
                full = nt(ext[h, near, :], other)
                for i in range(nb):
                    lanes = slice(i * BLOCK, (i + 1) * BLOCK)
                    own = full[(i + 1 - skip) * BLOCK : (i + 2 - skip) * BLOCK, lanes]
                    if i >= skip:
                        own = jnp.where(before, full[(i - skip) * BLOCK : (i + 1 - skip) * BLOCK, lanes], own)
                    held[h % AHEAD, :, pl.ds(t * TILE + i * BLOCK, BLOCK)] = own

    def spread(both):
        strips = []
        for j in range(nb + 1):
            cells = []
            for i in range(nb):
                lanes = slice(i * BLOCK, (i + 1) * BLOCK)
                cells.append(both[j - i][:, lanes] if 0 <= j - i <= 1 else none)
            strips.append(jnp.concatenate(cells, 1))
        return strips

    def softmaxed(h):
        gain = g[:, cols(h)]
        sk, sv = summary(h, 0), summary(h, 1)
        skT, kxT = sk.T, kx[h].T
        dsk = dsv = gp = None
        for t in range(length // TILE):
            rows = pl.ds(t * TILE, TILE)
            near = slice(t * TILE, t * TILE + (nb + 1) * BLOCK)
            scaled, grads = qs[h, rows, :], do[h, rows, :]
            bs, bd = sb[h % AHEAD, :, rows], db[h % AHEAD, :, rows]
            ss, sd = nt(sk, scaled), nt(sv, grads)
            slot = lax.broadcasted_iota(jnp.int32, (slots, TILE), 0)
            if t == 0:
                rs = nt(kx[h, pl.ds(0, BLOCK), :], scaled[:BLOCK])
                rd = nt(vx[h, pl.ds(0, BLOCK), :], grads[:BLOCK])
                rs = jnp.where(rank > 0, rs, NEG)
                bs = jnp.concatenate([jnp.where(before, rs, bs[:, :BLOCK]), bs[:, BLOCK:]], 1)
                bd = jnp.concatenate([jnp.where(before, rd, bd[:, :BLOCK]), bd[:, BLOCK:]], 1)
                spos = slot // SUMMARY * STRIDE + STRIDE - SUMMARY + slot % SUMMARY
                qpos = rank * length + lax.broadcasted_iota(jnp.int32, (slots, TILE), 1)
                seen = qpos - spos >= BLOCK
            else:
                seen = slot < SUMMARY * rank
            ss = jnp.where(seen, ss, NEG)
            top = jnp.maximum(jnp.max(bs, 0, keepdims=True), jnp.max(ss, 0, keepdims=True))
            eb = jnp.exp2((bs - top) * (SCALE * LOG2E))
            es = jnp.exp2((ss - top) * (SCALE * LOG2E))
            inv = 1.0 / (jnp.sum(eb, 0, keepdims=True) + jnp.sum(es, 0, keepdims=True))
            pb, ps = eb * inv, es * inv
            delta = jnp.sum(pb * bd, 0, keepdims=True) + jnp.sum(ps * sd, 0, keepdims=True)
            gb = pb * ((bd - delta) * SCALE)
            gs = (ps * ((sd - delta) * SCALE)).astype(bf16)
            ps = ps.astype(bf16)
            split = lambda x: (jnp.where(wide, x, 0.0).astype(bf16), jnp.where(wide, 0.0, x).astype(bf16))
            pb, gb = split(pb), split(gb)
            for i in range(2):
                pst[h, pl.ds(i * BLOCK, BLOCK), rows] = pb[i]
                gst[h, pl.ds(i * BLOCK, BLOCK), rows] = gb[i]
            pst[h, pl.ds(2 * BLOCK, slots), rows] = ps
            dsv, dsk = plus(dsv, nn(ps, grads)), plus(dsk, nn(gs, scaled))
            if t == 0:
                grim[h, 0] = nn(gb[0][:, :BLOCK], scaled[:BLOCK]).astype(bf16)
                grim[h, 1] = nn(pb[0][:, :BLOCK], grads[:BLOCK]).astype(bf16)
            dq = nn(
                jnp.concatenate([kxT[:, near], skT], 1), jnp.concatenate(spread(gb) + [gs], 0)
            ).T
            gq_ref[rows, cols(h)] = (dq * gain).astype(bf16)
            gp = plus(gp, jnp.sum(dq * q[h, rows, :].astype(f32), 0, keepdims=True))
        for which, x in enumerate((dsk, dsv)):
            gsum[:, which, :, cols(h)] = x.reshape(slots // SUMMARY, SUMMARY, HD).astype(bf16)
        gbuf[pl.ds(h, 1), :] = gp

    def attended(h):
        svT, vxT = summary(h, 1).T, vx[h].T
        dk, dv = [None] * (blocks + 1), [None] * (blocks + 1)
        for t in range(length // TILE):
            rows = pl.ds(t * TILE, TILE)
            near = slice(t * TILE, t * TILE + (nb + 1) * BLOCK)
            first = t * nb
            two = lambda ref: [ref[h, pl.ds(i * BLOCK, BLOCK), rows] for i in range(2)]
            prob = spread(two(pst))
            dscore = spread(two(gst))
            dvt = nn(jnp.concatenate(prob, 0), do[h, rows, :])
            dkt = nn(jnp.concatenate(dscore, 0), qs[h, rows, :])
            for j in range(nb + 1):
                strip = slice(j * BLOCK, (j + 1) * BLOCK)
                dv[first + j] = plus(dv[first + j], dvt[strip])
                dk[first + j] = plus(dk[first + j], dkt[strip])
            full = jnp.concatenate(prob + [pst[h, pl.ds(2 * BLOCK, slots), rows]], 0)
            o_ref[rows, cols(h)] = nn(jnp.concatenate([vxT[:, near], svT], 1), full).T.astype(bf16)
            for n in range(max(first, 1), first + nb):
                gk_ref[pl.ds((n - 1) * BLOCK, BLOCK), cols(h)] = dk[n].astype(bf16)
                gv_ref[pl.ds((n - 1) * BLOCK, BLOCK), cols(h)] = dv[n].astype(bf16)

        @pl.when(rank < ranks - 1)
        def _():
            grim_copy(h).wait_recv()

        later = rank < ranks - 1
        for which, (x, out) in enumerate(((dk[blocks], gk_ref), (dv[blocks], gv_ref))):
            x = x + jnp.where(later, rrim[h, which].astype(f32), 0.0)
            out[pl.ds(last, BLOCK), cols(h)] = x.astype(bf16)
            edge[which, :, cols(h)] = x[BLOCK - 16 :]

    own = [
        pltpu.make_async_copy(full.at[pl.ds(length - SUMMARY, SUMMARY), :], sums.at[rank, i], loc.at[i])
        for i, full in enumerate((k_all, v_all))
    ]
    gains = pltpu.make_async_copy(g_all, g, loc.at[2])
    gains.start()

    def start_load(h):
        for i in range(4):
            load_copy(h, i).start()

    start_load(0)
    for copy in own:
        copy.start()
    each(H, start_load, 1)

    @pl.when(rank == 0)
    def _():
        for i in range(H):
            kx[i, pl.ds(0, BLOCK), :] = jnp.zeros((BLOCK, HD), bf16)
            vx[i, pl.ds(0, BLOCK), :] = jnp.zeros((BLOCK, HD), bf16)

    barrier = pltpu.get_barrier_semaphore()

    def greet(**device):
        pl.semaphore_signal(barrier, inc=1, device_id=device, device_id_type=MESH)

    others(pairs, pair, lambda p: greet(ctx=p * 2 + side))
    others(cells, cell, lambda c: greet(dp=c // 2, ctx=pair * 2 + c % 2))
    beside = rank + 2 * side - 1
    inside = (beside >= 0) & (beside < ranks)

    @pl.when(inside)
    def _():
        greet(ctx=jnp.clip(beside, 0, ranks - 1))

    gains.wait()
    for copy in own:
        copy.wait()
    banded(0)
    pl.semaphore_wait(barrier, pairs - 1 + cells - 1 + inside.astype(jnp.int32))
    part_copy(rank).start()
    each(H, send_rim)

    def early(h):
        @pl.when(h == 2)
        def _():
            part_copy(partner).wait_recv()
            for group in range(groups):
                send_sums(group)

        banded(h)

    each(AHEAD, early, 1)

    def middle(h):
        for group in range(groups):

            @pl.when(h == OUTWARD[group])
            def _(group=group):
                each(pair, lambda s: sum_copy(group, s, pair).wait_recv())

        @pl.when(rank > 0)
        def _():
            for which in range(2):
                rim_copy(h, which).wait_recv()

        @pl.when(h >= AHEAD)
        def _():
            banded(h)

        softmaxed(h)

        @pl.when(rank > 0)
        def _():
            grim_copy(h).start()

        for part in range(parts):

            @pl.when(h == BACK[part + 1] - 1)
            def _(part=part):
                each(pair, lambda t: gsum_copy(part, pair, t).start())

    each(H, middle)
    others(cells, cell, lambda c: cell_copy(cell, c).start())

    def final(h):
        @pl.when(h == 2)
        def _():
            others(cells, cell, lambda c: cell_copy(c, cell).wait_recv())
            gsub[cell] = gbuf[...]
            total = gsub[0]
            for c in range(1, gsub.shape[0]):
                total = total + gsub[c]
            gsub[cell] = total
            gall[pair] = total
            others(pairs, pair, lambda p: pair_copy(pair, p).start())
            collect(range(EARLY), heads(BACK, 0, EARLY))
            gpart_copy(0).start()

        @pl.when(h == 4)
        def _():
            collect(range(EARLY, parts), heads(BACK, EARLY, parts))
            gpart_copy(1).start()

        attended(h)

    each(H, final)

    for group in range(groups):
        each(pairs, lambda t, group=group: sum_copy(group, pair, t).wait_send(), pair + 1)
    part_copy(rank).wait_send()

    @pl.when(rank < ranks - 1)
    def _():
        for i in range(H):
            for which in range(2):
                rim_copy(i, which).wait_send()

    @pl.when(rank > 0)
    def _():
        for i in range(H):
            grim_copy(i).wait_send()

    for part in range(parts):
        each(pair, lambda t, part=part: gsum_copy(part, pair, t).wait_send())
    for late in range(2):
        gpart_copy(late).wait_recv()
    for which, out in enumerate((gk_ref, gv_ref)):
        extra = acc[side, which] + racc[which]
        extra = jnp.concatenate([jnp.zeros((16 - SUMMARY, extra.shape[1]), f32), extra], 0)
        out[pl.ds(length - 16, 16), :] = (edge[which] + extra).astype(bf16)

    others(pairs, pair, lambda p: pair_copy(p, pair).wait_recv())
    total = gall[0]
    for p in range(1, gall.shape[0]):
        total = total + gall[p]
    gain_out[...] = total * (dps * ranks * length) ** -0.5
    others(cells, cell, lambda c: cell_copy(cell, c).wait_send())
    others(pairs, pair, lambda p: pair_copy(pair, p).wait_send())
    for late in range(2):
        gpart_copy(late).wait_send()


def write_kernel(o_in, gq_in, gk_in, gv_in, gain_in, o_out, gq_out, gk_out, gv_out, gain_out, sems):
    length = o_in.shape[0]
    moves = []
    for source, target in ((o_in, o_out), (gq_in, gq_out), (gk_in, gk_out), (gv_in, gv_out)):
        for i in range(2):
            rows = pl.ds(i * (length // 2), length // 2)
            moves.append((source.at[rows], target.at[rows]))
    copies = [pltpu.make_async_copy(a, b, sems.at[i]) for i, (a, b) in enumerate(moves)]
    for copy in copies:
        copy.start()
    for i in range(H):
        gain_out[:, i * HD : (i + 1) * HD] = gain_in[i : i + 1, :]
    for copy in copies:
        copy.wait()


def solution(mesh):
    dps, ranks = mesh.shape["dp"], mesh.shape["ctx"]

    def per_device(queries, keys, values, cotangent, gain):
        _, length, width = queries.shape
        flat = lambda x: x.reshape(length, width)
        q, k, v, do = flat(queries), flat(keys), flat(values), flat(cotangent)
        away = pl.BlockSpec(memory_space=pl.ANY)
        near = pl.BlockSpec(memory_space=pltpu.VMEM)
        far = pl.BlockSpec(memory_space=pltpu.HBM)
        like = jax.ShapeDtypeStruct
        dma = lambda *shape: pltpu.SemaphoreType.DMA(shape)
        groups, parts = len(OUTWARD) - 1, len(BACK) - 1
        slots = ranks * SUMMARY
        held = pl.pallas_call(
            exchange_kernel,
            name="attend_exchange",
            in_specs=[far] * 5,
            out_specs=[near] * 5,
            out_shape=[like((length, width), bf16)] * 4 + [like((H, HD), f32)],
            scratch_shapes=[
                pltpu.VMEM((H, length, HD), bf16),
                pltpu.VMEM((H, length, HD), bf16),
                pltpu.VMEM((H, length, HD), bf16),
                pltpu.VMEM((H, length + BLOCK, HD), bf16),
                pltpu.VMEM((H, length + BLOCK, HD), bf16),
                pltpu.VMEM((1, width), f32),
                pltpu.VMEM((AHEAD, BLOCK, length), f32),
                pltpu.VMEM((AHEAD, BLOCK, length), f32),
                pltpu.VMEM((H, 2 * BLOCK + slots, length), bf16),
                pltpu.VMEM((H, 2 * BLOCK, length), bf16),
                pltpu.VMEM((ranks, 2, SUMMARY, width), bf16),
                pltpu.VMEM((H, 2, BLOCK, HD), bf16),
                pltpu.VMEM((H, 2, BLOCK, HD), bf16),
                pltpu.VMEM((ranks, 2, SUMMARY, width), bf16),
                pltpu.VMEM((ranks // 2, 2, 2, SUMMARY, width), bf16),
                pltpu.VMEM((2, 16, width), f32),
                pltpu.VMEM((2, 2, SUMMARY, width), f32),
                pltpu.VMEM((2, SUMMARY, width), f32),
                pltpu.VMEM((H, HD), f32),
                pltpu.VMEM((dps * 2, H, HD), f32),
                pltpu.VMEM((ranks // 2, H, HD), f32),
                dma(H, 2), dma(H, 2),
                pltpu.SemaphoreType.DMA, pltpu.SemaphoreType.DMA,
                dma(groups, ranks // 2), dma(groups, ranks // 2),
                dma(H), dma(H),
                dma(parts, ranks // 2), dma(parts, ranks // 2),
                dma(2), dma(2),
                dma(dps * 2), dma(dps * 2),
                dma(ranks // 2), dma(ranks // 2),
                dma(3), dma(H, 4),
            ],
            compiler_params=pltpu.CompilerParams(
                collective_id=0, has_side_effects=True, vmem_limit_bytes=44 << 20
            ),
        )(q, do, k, v, gain.reshape(1, width))
        out = pl.pallas_call(
            write_kernel,
            name="attend_write",
            in_specs=[away] * 4 + [near],
            out_specs=[away] * 4 + [near],
            out_shape=[like((length, width), bf16)] * 4 + [like((1, width), f32)],
            scratch_shapes=[dma(8)],
            compiler_params=pltpu.CompilerParams(vmem_limit_bytes=2 << 20),
        )(*held)
        whole = lambda x: x.reshape(1, length, width)
        return whole(out[0]), whole(out[1]), whole(out[2]), whole(out[3]), out[4].reshape(width)

    spread = P("dp", "ctx", None)
    return jax.shard_map(
        per_device,
        mesh=mesh,
        in_specs=(spread,) * 4 + (P(),),
        out_specs=(spread,) * 4 + (P(),),
        check_vma=False,
    )
```

time: 67.6 us -> 70.6 us (1.044); the launches traced: 67.3 us -> 69.2 us
  Pallas kernels: 66 us -> 67.9 us
    pallas_call x2, Pallas kernels: 66 us -> 67.9 us  [the longest x1 63.9 us: per_device(): pl.pallas_call(exchange_kernel, name='attend_exchange', in_specs=[far] *...]
where the time goes in v4:
time: 70.6 us; the launch traced here: 69.2 us
  Pallas kernels  67.9 us (96%)
    pallas_call x1, Pallas kernels, per_device(): pl.pallas_call(exchange_kernel, name='attend_exchange', in_specs=[far] *...  63.9 us
    pallas_call x1, Pallas kernels, per_device(): pl.pallas_call(write_kernel, name='attend_write', in_specs=[away] * 4 + [...  3.96 us

profile of v4, /device:TPU:1, one launch (start us, length us, event | category | flops | bytes accessed | tf_op | source)
XLA Modules:
  0.0 69.2 jit_solution(1537083880470418877)
XLA Ops:
  0.6 0.0 copy-start
  0.6 0.7 copy-done
  1.3 63.9 %attend_exchange.1 = (bf16[1024,1024]{1,0:T(8,128)(2,1)S(1)}, bf16[1024,1024]{1,0:T(8,128)(2,1)S(1)}, bf16[1024,1024]{1,0:T(8,128)(2,1)S(1)}, bf16[1024,1024]{1,0:T(8,128)(2,1)S(1)}, f32[8,128]{1,0:T(8,128)S(1)}) custom-call(bf16[1024,1024]{1,0:T(8,128)(2,1)} %bitcast.11, bf16[1024,1024]{1,0:T(8,128)(2,1)} %bitcast.12, bf16[1024,1024]{1,0:T(8,128)(2,1)} %bitcast.13, ...), custom_call_target="tpu_custom_call" | custom-call | tf_op jit(solution)/shard_map/attend_exchange/pallas_call | solution.py:449
  65.3 4.0 %attend_write.1 = (bf16[1024,1024]{1,0:T(8,128)(2,1)}, bf16[1024,1024]{1,0:T(8,128)(2,1)}, bf16[1024,1024]{1,0:T(8,128)(2,1)}, bf16[1024,1024]{1,0:T(8,128)(2,1)}, f32[1,1024]{1,0:T(1,128)}) custom-call(bf16[1024,1024]{1,0:T(8,128)(2,1)S(1)} %get-tuple-element.15.o_in, bf16[1024,1024]{1,0:T(8,128)(2,1)S(1)} %get-tuple-element.16.gq_in, ...), custom_call_target="tpu_custom_call" | custom-call | tf_op jit(solution)/shard_map/attend_write/pallas_call | solution.py:491
Async XLA Ops:
  0.6 0.7 copy-start

commit v5 on v4

--- a/solution.py
+++ b/solution.py
@@ -18,10 +18,12 @@
 LOG2E = 1.4426950408889634
 NEG = -1e30
 TILE = 256
-OUTWARD = (0, 1, 3, 8)
-BACK = (0, 3, 6, 8)
+OUTWARD = (0, 1, 2, 4, 6, 8)
+OUT_AT = (-1, -1, 0, 2, 4)
+BACK = (0, 4, 7, 8)
 EARLY = 2
-AHEAD = 4
+AHEAD = 3
+LAG = 4
 
 
 def nt(a, b):
@@ -314,20 +316,27 @@
     banded(0)
     pl.semaphore_wait(barrier, pairs - 1 + cells - 1 + inside.astype(jnp.int32))
     part_copy(rank).start()
-    each(H, send_rim)
-
-    def early(h):
-        @pl.when(h == 2)
-        def _():
-            part_copy(partner).wait_recv()
-            for group in range(groups):
-                send_sums(group)
-
-        banded(h)
-
-    each(AHEAD, early, 1)
+    send_rim(0)
+    banded(1)
+    part_copy(partner).wait_recv()
+    for group in range(groups):
+        if OUT_AT[group] < 0:
+            send_sums(group)
+    send_rim(1)
+    each(AHEAD, banded, 2)
 
     def middle(h):
+        @pl.when(h + 2 < H)
+        def _():
+            send_rim(h + 2)
+
+        for group in range(groups):
+            if OUT_AT[group] >= 0:
+
+                @pl.when(h == OUT_AT[group])
+                def _(group=group):
+                    send_sums(group)
+
         for group in range(groups):
 
             @pl.when(h == OUTWARD[group])
@@ -339,10 +348,6 @@
             for which in range(2):
                 rim_copy(h, which).wait_recv()
 
-        @pl.when(h >= AHEAD)
-        def _():
-            banded(h)
-
         softmaxed(h)
 
         @pl.when(rank > 0)
@@ -355,11 +360,21 @@
             def _(part=part):
                 each(pair, lambda t: gsum_copy(part, pair, t).start())
 
+        @pl.when(h == H - 1)
+        def _():
+            others(cells, cell, lambda c: cell_copy(cell, c).start())
+
+        @pl.when(h + AHEAD < H)
+        def _():
+            banded(h + AHEAD)
+
+        @pl.when(h >= LAG)
+        def _():
+            attended(h - LAG)
+
     each(H, middle)
-    others(cells, cell, lambda c: cell_copy(cell, c).start())
-
     def final(h):
-        @pl.when(h == 2)
+        @pl.when(h == H - LAG + 1)
         def _():
             others(cells, cell, lambda c: cell_copy(c, cell).wait_recv())
             gsub[cell] = gbuf[...]
@@ -372,14 +387,14 @@
             collect(range(EARLY), heads(BACK, 0, EARLY))
             gpart_copy(0).start()
 
-        @pl.when(h == 4)
+        @pl.when(h == H - LAG + 2)
         def _():
             collect(range(EARLY, parts), heads(BACK, EARLY, parts))
             gpart_copy(1).start()
 
         attended(h)
 
-    each(H, final)
+    each(H, final, H - LAG)
 
     for group in range(groups):
         each(pairs, lambda t, group=group: sum_copy(group, pair, t).wait_send(), pair + 1)

time: 70.6 us -> 63.1 us (0.89); the launches traced: 69.2 us -> 62.9 us
  Pallas kernels: 67.9 us -> 61.6 us
    pallas_call x1, Pallas kernels: 63.9 us -> 57.6 us  [per_device(): pl.pallas_call(exchange_kernel, name='attend_exchange', in_specs=[far] *...]
where the time goes in v5:
time: 63.1 us; the launch traced here: 62.9 us
  Pallas kernels  61.6 us (98%)
  local copies, waits for them, and re-layouts  0.68 us (1%)
  between operations  0.65 us (1%)
    pallas_call x1, Pallas kernels, per_device(): pl.pallas_call(exchange_kernel, name='attend_exchange', in_specs=[far] *...  57.6 us
    pallas_call x1, Pallas kernels, per_device(): pl.pallas_call(write_kernel, name='attend_write', in_specs=[away] * 4 + [...  3.96 us

profile of v5, /device:TPU:1, one launch (start us, length us, event | category | flops | bytes accessed | tf_op | source)
XLA Modules:
  0.0 62.9 jit_solution(5210334819860407364)
XLA Ops:
  0.6 0.0 copy-start
  0.6 0.7 %copy-done = f32[1024]{0:T(1024)S(1)} copy-done((f32[1024]{0:T(1024)S(1)}, f32[1024]{0:T(1024)}, u32[]{:S(2)}) %copy-start) | copy-done | bytes 4120
  1.3 57.6 %attend_exchange.1 = (bf16[1024,1024]{1,0:T(8,128)(2,1)S(1)}, bf16[1024,1024]{1,0:T(8,128)(2,1)S(1)}, bf16[1024,1024]{1,0:T(8,128)(2,1)S(1)}, bf16[1024,1024]{1,0:T(8,128)(2,1)S(1)}, f32[8,128]{1,0:T(8,128)S(1)}) custom-call(bf16[1024,1024]{1,0:T(8,128)(2,1)} %bitcast.11, bf16[1024,1024]{1,0:T(8,128)(2,1)} %bitcast.12, bf16[1024,1024]{1,0:T(8,128)(2,1)} %bitcast.13, ...), custom_call_target="tpu_custom_call" | custom-call | tf_op jit(solution)/shard_map/attend_exchange/pallas_call | solution.py:464
  59.0 4.0 %attend_write.1 = (bf16[1024,1024]{1,0:T(8,128)(2,1)}, bf16[1024,1024]{1,0:T(8,128)(2,1)}, bf16[1024,1024]{1,0:T(8,128)(2,1)}, bf16[1024,1024]{1,0:T(8,128)(2,1)}, f32[1,1024]{1,0:T(1,128)}) custom-call(bf16[1024,1024]{1,0:T(8,128)(2,1)S(1)} %get-tuple-element.15.o_in, bf16[1024,1024]{1,0:T(8,128)(2,1)S(1)} %get-tuple-element.16.gq_in, ...), custom_call_target="tpu_custom_call" | custom-call | tf_op jit(solution)/shard_map/attend_write/pallas_call | solution.py:506
Async XLA Ops:
  0.6 0.7 %copy-start = (f32[1024]{0:T(1024)S(1)}, f32[1024]{0:T(1024)}, u32[]{:S(2)}) copy-start(f32[1024]{0:T(1024)} %param.9) | copy-start | bytes 12292

commit v6 on v5

--- a/solution.py
+++ b/solution.py
@@ -24,6 +24,7 @@
 EARLY = 2
 AHEAD = 3
 LAG = 4
+LEAD = 3
 
 
 def nt(a, b):
@@ -317,18 +318,20 @@
     pl.semaphore_wait(barrier, pairs - 1 + cells - 1 + inside.astype(jnp.int32))
     part_copy(rank).start()
     send_rim(0)
+    send_rim(1)
     banded(1)
     part_copy(partner).wait_recv()
     for group in range(groups):
         if OUT_AT[group] < 0:
             send_sums(group)
-    send_rim(1)
+    for i in range(2, LEAD):
+        send_rim(i)
     each(AHEAD, banded, 2)
 
     def middle(h):
-        @pl.when(h + 2 < H)
-        def _():
-            send_rim(h + 2)
+        @pl.when(h + LEAD < H)
+        def _():
+            send_rim(h + LEAD)
 
         for group in range(groups):
             if OUT_AT[group] >= 0:

time: 63.1 us -> 69.3 us (1.098); the launches traced: 62.9 us -> 67.9 us
  Pallas kernels: 61.6 us -> 66.6 us
    pallas_call x1, Pallas kernels: 57.6 us -> 62.6 us  [per_device(): pl.pallas_call(exchange_kernel, name='attend_exchange', in_specs=[far] *...]
where the time goes in v6:
time: 69.3 us; the launch traced here: 67.9 us
  Pallas kernels  66.6 us (96%)
    pallas_call x1, Pallas kernels, per_device(): pl.pallas_call(exchange_kernel, name='attend_exchange', in_specs=[far] *...  62.6 us
    pallas_call x1, Pallas kernels, per_device(): pl.pallas_call(write_kernel, name='attend_write', in_specs=[away] * 4 + [...  3.96 us

profile of v6, /device:TPU:1, one launch (start us, length us, event | category | flops | bytes accessed | tf_op | source)
XLA Modules:
  0.0 67.9 jit_solution(13209455604434402641)
XLA Ops:
  0.6 0.0 copy-start
  0.6 0.7 copy-done
  1.3 62.6 %attend_exchange.1 = (bf16[1024,1024]{1,0:T(8,128)(2,1)S(1)}, bf16[1024,1024]{1,0:T(8,128)(2,1)S(1)}, bf16[1024,1024]{1,0:T(8,128)(2,1)S(1)}, bf16[1024,1024]{1,0:T(8,128)(2,1)S(1)}, f32[8,128]{1,0:T(8,128)S(1)}) custom-call(bf16[1024,1024]{1,0:T(8,128)(2,1)} %bitcast.11, bf16[1024,1024]{1,0:T(8,128)(2,1)} %bitcast.12, bf16[1024,1024]{1,0:T(8,128)(2,1)} %bitcast.13, ...), custom_call_target="tpu_custom_call" | custom-call | tf_op jit(solution)/shard_map/attend_exchange/pallas_call | solution.py:467
  64.0 4.0 %attend_write.1 = (bf16[1024,1024]{1,0:T(8,128)(2,1)}, bf16[1024,1024]{1,0:T(8,128)(2,1)}, bf16[1024,1024]{1,0:T(8,128)(2,1)}, bf16[1024,1024]{1,0:T(8,128)(2,1)}, f32[1,1024]{1,0:T(1,128)}) custom-call(bf16[1024,1024]{1,0:T(8,128)(2,1)S(1)} %get-tuple-element.15.o_in, bf16[1024,1024]{1,0:T(8,128)(2,1)S(1)} %get-tuple-element.16.gq_in, ...), custom_call_target="tpu_custom_call" | custom-call | tf_op jit(solution)/shard_map/attend_write/pallas_call | solution.py:509
Async XLA Ops:
  0.6 0.7 %copy-start = (f32[1024]{0:T(1024)S(1)}, f32[1024]{0:T(1024)}, u32[]{:S(2)}) copy-start(f32[1024]{0:T(1024)} %param.9) | copy-start | bytes 12292
